TPU v7x, 32 devices: a whole 2x2x4 slice. The times are simulated.
32 devices in a mesh: dp: 2 (over core), row: 4 (over y, x), col: 4 (over z).
Axes of the slice: x: 2, y: 2, z: 4, core: 2. Of those that a mesh axis runs over, the one named last changes fastest.
Arguments:
- tokens: bfloat16 [8192, 1024], P(('dp', 'row'), 'col'), may hold values from -6 to 6
- segment_ids: int32 [16, 512], P(('dp', 'col')), may hold values from 0 to 7, never falling along the last dimension, each value on 1 to 256 neighbouring positions
- gain_attn: float32 [1024], P('col'), may hold values from 0.5 to 1.5
- gain_ffn: float32 [1024], P('col'), may hold values from 0.5 to 1.5
- w_qkv: bfloat16 [1024, 3, 1024], P('col', None, 'row'), may hold values from -0.1875 to 0.1875
- w_out: bfloat16 [1024, 1024], P('row', 'col'), may hold values from -1 to 1
- w_gate_up: bfloat16 [1024, 2, 2816], P('col', None, 'row'), may hold values from -0.1875 to 0.1875
- w_down: bfloat16 [2816, 1024], P('row', 'col'), may hold values from -0.109375 to 0.109375
- grad_out: bfloat16 [8192, 1024], P(('dp', 'row'), 'col'), may hold values from -6 to 6
Outputs:
- output: bfloat16 [8192, 1024], P(('dp', 'row'), 'col')
- grad_tokens: float32 [8192, 1024], P(('dp', 'row'), 'col')
- grad_gain_attn: float32 [1024], P('col')
- grad_gain_ffn: float32 [1024], P('col')
- grad_w_qkv: float32 [1024, 3, 1024], P('col', None, 'row')
- grad_w_out: float32 [1024, 1024], P('row', 'col')
- grad_w_gate_up: float32 [1024, 2, 2816], P('col', None, 'row')
- grad_w_down: float32 [2816, 1024], P('row', 'col')
Inputs may be any that keep to these rules, and one draw needn't show every extreme that they name: `segment_ids`: in each sequence the ids never fall along its 512 positions; each of the 8 ids covers 1 to 256 consecutive positions.
All inputs are finite; a program needn't handle non-finite values.
Results may differ from a plain program's by a relative error of at most 0.013.
The roundings to bfloat16 on the way count: a program that leaves them out, or rounds other values in their place, can miss the bound.
Values may be sent and summed in bfloat16 or wider, within the bound.
No kernel may reach another device: no remote copies, remote signals or barrier semaphores. Data moves between devices by JAX's collectives and lax.ppermute only.
A program may use at most 256 MiB of HBM per device.

v0:
```python
import jax
import jax.numpy as jnp
from jax import lax
from jax.experimental import pallas as pl
from jax.experimental.pallas import tpu as pltpu
from jax.sharding import PartitionSpec as P

D = 1024
HEAD_DIM = 64


EPS = 1e-06
MASKED = -1e30


def row_norm(values, gain_vec):
    squares = lax.psum(jnp.sum(values * values, axis=1), "col")
    rescale = lax.rsqrt(squares / D + EPS)
    unit_rows = values * rescale[:, None]
    return (unit_rows, rescale, (unit_rows * gain_vec[None, :]).astype(jnp.bfloat16))


def norm_backward(grad_normed, unit_rows, rescale, gain_vec):
    weighted = grad_normed * gain_vec[None, :]
    inner_sum = lax.psum(jnp.sum(weighted * unit_rows, axis=1), "col")
    grad_in = rescale[:, None] * (weighted - unit_rows * (inner_sum / D)[:, None])
    grad_gain = jnp.sum(grad_normed * unit_rows, axis=0)
    return (grad_in, grad_gain)


def project_up(normed, weight_block):
    gathered = lax.all_gather(normed, "row", axis=0, tiled=True)

    def term(begin_at):
        return jnp.dot(gathered, weight_block, preferred_element_type=jnp.float32)

    result = lax.psum_scatter(
        term(jnp.int32(0)),
        "col",
        scatter_dimension=0,
        tiled=True,
    )
    return (gathered, result.astype(jnp.bfloat16))


def project_down(values, weight_block):
    gathered = lax.all_gather(values, "col", axis=0, tiled=True)

    def term(begin_at):
        return jnp.dot(gathered, weight_block, preferred_element_type=jnp.float32)

    result = lax.psum_scatter(
        term(jnp.int32(0)),
        "row",
        scatter_dimension=0,
        tiled=True,
    )
    return (gathered, result)


def back_down(grad_rows, weight_block):
    gathered = lax.all_gather(grad_rows, "row", axis=0, tiled=True)

    def term(begin_at):
        return lax.dot_general(
            gathered, weight_block, (((1,), (1,)), ((), ())), preferred_element_type=jnp.float32
        )

    result = lax.psum_scatter(
        term(jnp.int32(0)),
        "col",
        scatter_dimension=0,
        tiled=True,
    )
    return (gathered, result.astype(jnp.bfloat16))


def back_up(grad_cols, weight_block):
    gathered = lax.all_gather(grad_cols, "col", axis=0, tiled=True)

    def term(begin_at):
        return lax.dot_general(
            gathered, weight_block, (((1,), (1,)), ((), ())), preferred_element_type=jnp.float32
        )

    result = lax.psum_scatter(
        term(jnp.int32(0)),
        "row",
        scatter_dimension=0,
        tiled=True,
    )
    return (gathered, result)


def weight_grad(left_rows, right_rows):
    return lax.dot_general(
        left_rows, right_rows, (((0,), (0,)), ((), ())), preferred_element_type=jnp.float32
    )


def block_scores(queries, keys_all, query_segment, key_segment, query_place):
    raw = jnp.einsum(
        "qhd,khd->hqk", queries, keys_all, preferred_element_type=jnp.float32
    ) * HEAD_DIM ** (-0.5)
    key_place = lax.broadcasted_iota(jnp.int32, (1, keys_all.shape[0]), 1)
    allowed = (query_segment[:, None] == key_segment[None, :]) & (key_place <= query_place[:, None])
    return jnp.where(allowed[None], raw, MASKED)


def split_blocks(queries, segment):
    length = queries.shape[0]
    block_rows = min(512, length)
    blocks = length // block_rows
    place = jnp.arange(length, dtype=jnp.int32).reshape(blocks, block_rows)
    return (
        queries.reshape(blocks, block_rows, queries.shape[1], queries.shape[2]),
        segment.reshape(blocks, block_rows),
        place,
    )


def attend_forward(queries, keys_all, values_all, segment):
    query_blocks, segment_blocks, place_blocks = split_blocks(queries, segment)

    def one_block(item):
        query_rows, query_segment, query_place = item
        scores = block_scores(query_rows, keys_all, query_segment, segment, query_place)
        row_max = jnp.max(scores, axis=-1, keepdims=True)
        expo = jnp.exp(scores - row_max)
        row_total = jnp.sum(expo, axis=-1, keepdims=True)
        prob_rows = (expo / row_total).astype(jnp.bfloat16)
        mixed = jnp.einsum(
            "hqk,khd->qhd", prob_rows, values_all, preferred_element_type=jnp.float32
        )
        return (mixed, row_max[..., 0] + jnp.log(row_total[..., 0]))

    mixed, log_total = lax.map(one_block, (query_blocks, segment_blocks, place_blocks))
    return (mixed.reshape(queries.shape[0], -1).astype(jnp.bfloat16), log_total)


def attend_backward(queries, keys_all, values_all, segment, log_total, grad_mix):
    query_blocks, segment_blocks, place_blocks = split_blocks(queries, segment)
    grad_blocks = grad_mix.reshape(query_blocks.shape)
    factor = HEAD_DIM ** (-0.5)

    def one_block(carry, item):
        key_acc, value_acc = carry
        query_rows, query_segment, query_place, log_rows, grad_rows = item
        scores = block_scores(query_rows, keys_all, query_segment, segment, query_place)
        prob_rows = jnp.exp(scores - log_rows[..., None])
        value_acc = value_acc + jnp.einsum(
            "hqk,qhd->khd",
            prob_rows.astype(jnp.bfloat16),
            grad_rows,
            preferred_element_type=jnp.float32,
        )
        grad_prob = jnp.einsum(
            "qhd,khd->hqk", grad_rows, values_all, preferred_element_type=jnp.float32
        )
        grad_scores = (
            prob_rows * (grad_prob - jnp.sum(prob_rows * grad_prob, axis=-1, keepdims=True))
        ).astype(jnp.bfloat16)
        grad_query = (
            jnp.einsum("hqk,khd->qhd", grad_scores, keys_all, preferred_element_type=jnp.float32)
            * factor
        )
        key_acc = (
            key_acc
            + jnp.einsum(
                "hqk,qhd->khd", grad_scores, query_rows, preferred_element_type=jnp.float32
            )
            * factor
        )
        return ((key_acc, value_acc), grad_query)

    zeros_like_keys = jnp.zeros(keys_all.shape, jnp.float32)
    (grad_keys, grad_values), grad_queries = lax.scan(
        one_block,
        (zeros_like_keys, zeros_like_keys),
        (query_blocks, segment_blocks, place_blocks, log_total, grad_blocks),
    )
    grad_queries = grad_queries.reshape(queries.shape)
    return jnp.stack([grad_queries, grad_keys, grad_values], axis=1).astype(jnp.bfloat16)


def local(tokens, segment_ids, gain_attn, gain_ffn, w_qkv, w_out, w_gate_up, w_down, grad_out):
    values = tokens.astype(jnp.float32)
    head_cols = w_qkv.shape[2]
    heads_here = head_cols // HEAD_DIM
    hidden_here = w_gate_up.shape[2]
    qkv_block = w_qkv.reshape(w_qkv.shape[0], 3 * head_cols)
    gate_up_block = w_gate_up.reshape(w_gate_up.shape[0], 2 * hidden_here)
    seq_count, seq_length = segment_ids.shape
    unit_one, rescale_one, normed_one = row_norm(values, gain_attn)
    gathered_one, packed = project_up(normed_one, qkv_block)
    packed = packed.reshape(-1, 3, heads_here, HEAD_DIM)
    mix_parts, log_parts = ([], [])
    for index in range(seq_count):
        rows_here = packed[index * seq_length : (index + 1) * seq_length]
        mixed, log_total = attend_forward(
            rows_here[:, 0], rows_here[:, 1], rows_here[:, 2], segment_ids[index]
        )
        mix_parts.append(mixed)
        log_parts.append(log_total)
    attn_mix = jnp.concatenate(mix_parts, axis=0)
    gathered_mix, attn_branch = project_down(attn_mix, w_out)
    hidden = values + attn_branch
    unit_two, rescale_two, normed_two = row_norm(hidden, gain_ffn)
    gathered_two, gate_up = project_up(normed_two, gate_up_block)
    gate_vals = gate_up[:, :hidden_here].astype(jnp.float32)
    up_vals = gate_up[:, hidden_here:].astype(jnp.float32)
    sigmoid_gate = jax.nn.sigmoid(gate_vals)
    silu_gate = gate_vals * sigmoid_gate
    active = (silu_gate * up_vals).astype(jnp.bfloat16)
    gathered_act, ffn_branch = project_down(active, w_down)
    output = (hidden + ffn_branch).astype(jnp.bfloat16)
    grad_rows_out, grad_active = back_down(grad_out, w_down)
    grad_down = weight_grad(gathered_act, grad_rows_out)
    grad_act_f = grad_active.astype(jnp.float32)
    grad_gate = grad_act_f * up_vals * sigmoid_gate * (1.0 + gate_vals * (1.0 - sigmoid_gate))
    grad_up = grad_act_f * silu_gate
    grad_gate_up_rows = jnp.concatenate([grad_gate, grad_up], axis=1).astype(jnp.bfloat16)
    grad_cols_two, grad_normed_two = back_up(grad_gate_up_rows, gate_up_block)
    grad_gate_up = weight_grad(gathered_two, grad_cols_two).reshape(w_gate_up.shape)
    grad_hidden_norm, grad_gain_two = norm_backward(
        grad_normed_two, unit_two, rescale_two, gain_ffn
    )
    grad_hidden = grad_out.astype(jnp.float32) + grad_hidden_norm
    grad_rows_hidden, grad_mix = back_down(grad_hidden.astype(jnp.bfloat16), w_out)
    grad_out_weight = weight_grad(gathered_mix, grad_rows_hidden)
    grad_mix = grad_mix.reshape(-1, heads_here, HEAD_DIM)
    grad_parts = []
    for index in range(seq_count):
        rows_here = packed[index * seq_length : (index + 1) * seq_length]
        grad_parts.append(
            attend_backward(
                rows_here[:, 0],
                rows_here[:, 1],
                rows_here[:, 2],
                segment_ids[index],
                log_parts[index],
                grad_mix[index * seq_length : (index + 1) * seq_length],
            )
        )
    grad_packed = jnp.concatenate(grad_parts, axis=0).reshape(-1, 3 * head_cols)
    grad_cols_one, grad_normed_one = back_up(grad_packed, qkv_block)
    grad_qkv = weight_grad(gathered_one, grad_cols_one).reshape(w_qkv.shape)
    grad_input_norm, grad_gain_one = norm_backward(
        grad_normed_one, unit_one, rescale_one, gain_attn
    )
    grad_tokens = grad_hidden + grad_input_norm
    summed = lax.psum((grad_qkv, grad_out_weight, grad_gate_up, grad_down), "dp")
    gains = lax.psum((grad_gain_one, grad_gain_two), ("dp", "row"))
    return (output, grad_tokens, gains[0], gains[1], summed[0], summed[1], summed[2], summed[3])


def swap(values):
    return lax.ppermute(values, "dp", [(0, 1), (1, 0)])


def hop(values, axis, flip):
    return lax.ppermute(values, axis, [(at, at ^ flip) for at in range(lax.axis_size(axis))])


def after(values, first):
    return lax.optimization_barrier((values, first))[0]


def by_core(core, mine, other, axis=0):
    first = jnp.where(core == 0, mine, other)
    second = jnp.where(core == 0, other, mine)
    return jnp.concatenate([first, second], axis=axis)


def pick(values, core, axis=0):
    half = values.shape[axis] // 2
    return lax.dynamic_slice_in_dim(values, core * half, half, axis)


def send_chunks(values, core, col, seq_length):
    seqs = values.shape[0] // seq_length
    parts = values.reshape(seqs, seq_length, -1)
    mine = pick(parts, core, 1)
    other = swap(pick(parts, 1 - core, 1))
    chunks = by_core(core, mine, other)
    got = []
    for flip in range(4):
        chunk = lax.dynamic_index_in_dim(chunks, col ^ flip, 0, keepdims=False)
        got.append(hop(chunk, "col", flip) if flip else chunk)
    return got


def to_sequence(got, core):
    rows = jnp.concatenate(got, axis=1)
    return by_core(core, rows, swap(rows))


def send_rows(rows):
    width = rows.shape[1] // 4
    parts = [rows[:, at * width : (at + 1) * width] for at in range(4)]
    return [parts[0]] + [hop(parts[flip], "col", flip) for flip in range(1, 4)]


def from_sequence(got, core, col, seq_length):
    got = jnp.stack(got, axis=0)
    seqs = 2

    def of_core(which):
        picked = [
            lax.dynamic_index_in_dim(got, (which * seqs + at) ^ col, 0, False) for at in range(seqs)
        ]
        return jnp.stack(picked)

    mine, other = (of_core(core), of_core(1 - core))
    return by_core(core, mine, swap(other), 1).reshape(seqs * seq_length, -1)


def times(left, right):
    return jnp.dot(left, right, preferred_element_type=jnp.float32)


def times_t(left, right):
    return lax.dot_general(
        left, right, (((1,), (1,)), ((), ())), preferred_element_type=jnp.float32
    )


def norm_rows(values):
    rescale = lax.rsqrt(jnp.mean(values * values, axis=1) + EPS)[:, None]
    return (values * rescale, rescale)


def norm_rows_back(grad_normed, unit_rows, rescale, gain_vec):
    weighted = grad_normed * gain_vec[None, :]
    inner = jnp.sum(weighted * unit_rows, axis=1, keepdims=True) / D
    return rescale * (weighted - unit_rows * inner)


def join_blocks(*refs):
    blocks, wholes = (refs[:16], refs[16:])
    _, rows, width = blocks[0].shape
    for at, block in enumerate(blocks):
        line, place = divmod(at, 4)
        kind = 0
        for whole in wholes:
            part = block[kind : kind + whole.shape[0]]
            kind += whole.shape[0]
            whole[:, line * rows : (line + 1) * rows, place * width : (place + 1) * width] = part


def spread_weights(block, first_cols=None, first_rows=None):
    grid = [[None] * 4 for _ in range(4)]
    block_cols = block if first_cols is None else after(block, first_cols)
    block_rows = block if first_rows is None else after(block, first_rows)
    near = hop(block_cols, "col", 1)
    far = hop(block_cols, "col", 3)
    grid[0] = [block_rows, near, hop(near, "col", 3), far]
    for at in (0, 1, 3, 2):
        grid[1][at] = hop(grid[0][at], "row", 1)
        grid[2][at] = hop(grid[0][at], "row", 2)
    for at in range(4):
        if at < 2:
            grid[3][at] = hop(grid[1][at], "row", 2)
        else:
            grid[3][at] = hop(grid[2][at], "row", 1)
    return grid


def join_weights(grid, splits):
    _, rows, width = grid[0][0].shape
    shapes = [jax.ShapeDtypeStruct((at, 4 * rows, 4 * width), jnp.bfloat16) for at in splits]
    wholes = pl.pallas_call(join_blocks, out_shape=shapes)(*[b for line in grid for b in line])
    return [whole.reshape(-1, 4 * width) for whole in wholes]


def wide(values):
    return values.astype(jnp.float32)


def low(values):
    return values.astype(jnp.bfloat16)


def start_rows(grad, kinds):
    grid = low(grad).reshape(kinds, 2, 2, -1, grad.shape[1])
    half = grad.shape[1] // 2
    left, right = (grid[..., :half], grid[..., half:])
    got = hop(left[:, 1], "row", 2)
    got_r = hop(right[:, :, 1], "row", 1)
    return (left, right, got, got_r)


def middle_rows(state):
    left, right, got, got_r = state
    sent = low(wide(left[:, 0, 1]) + wide(got[:, 1]))
    sent_r = low(wide(right[:, 1, 0]) + wide(got_r[:, 1]))
    return ((sent, sent_r), state + (hop(sent, "row", 1), hop(sent_r, "row", 2)))


def end_rows(state):
    left, right, got, got_r, last, last_r = state
    sums = wide(left[:, 0, 0]) + wide(got[:, 0]) + wide(last)
    sums_r = wide(right[:, 0, 0]) + wide(got_r[:, 0]) + wide(last_r)
    return (sums, sums_r)


def relay_cols(parts):
    own, first, second, third = parts
    got = hop(jnp.stack([third, second]), "col", 3)
    return (own, first, got)


def relay_last(state):
    own, first, got = state
    sent = low(wide(first) + wide(got[1]))
    return (sent, (own, got[0], hop(sent, "col", 1)))


def relay_sum(state):
    own, got, last = state
    return wide(own) + wide(got) + wide(last)


def split_cols(state):
    sums, sums_r = state
    width = sums.shape[-1] // 2
    parts = [low(sums[..., width:]), low(sums_r[..., :width]), low(sums_r[..., width:])]
    return [sums[..., :width]] + parts


def send_cols(parts):
    return [hop(parts[flip], "col", flip) for flip in (1, 2, 3)]


def end_cols(total, got):
    return total + wide(got[0]) + wide(got[1]) + wide(got[2])


def start_cols(grad):
    width = grad.shape[1] // 4
    return relay_cols([low(grad[:, at * width : (at + 1) * width]) for at in range(4)])


def join_halves(core_ref, mine, other, whole):
    rows = mine.shape[1]
    for at in range(2):
        part = slice(at * rows, (at + 1) * rows)

        @pl.when(core_ref[0] == at)
        def _():
            whole[:, part, :] = mine[...]

        @pl.when(core_ref[0] != at)
        def _():
            whole[:, part, :] = other[...].astype(jnp.float32)


def joined(mine, core):
    kinds, rows, width = mine.shape
    mine_low = low(mine)
    vmem = pl.BlockSpec(memory_space=pltpu.VMEM)
    return pl.pallas_call(
        join_halves,
        out_shape=jax.ShapeDtypeStruct((kinds, 2 * rows, width), jnp.float32),
        in_specs=[pl.BlockSpec(memory_space=pltpu.SMEM), vmem, vmem],
        out_specs=vmem,
    )(core[None], mine, swap(mine_low))


def chip_local(tokens, segment_ids, gain_attn, gain_ffn, w_qkv, w_out, w_gate_up, w_down, grad_out):
    core = lax.axis_index("dp")
    col = lax.axis_index("col")
    length = segment_ids.shape[1]
    features = w_qkv.shape[0]
    head_cols = w_qkv.shape[2] // 2
    heads = 4 * head_cols // HEAD_DIM
    factor = HEAD_DIM ** (-0.5)

    token_chunks = send_chunks(tokens, core, col, length)
    attn_block = jnp.concatenate(
        [pick(w_qkv, core, 2).transpose(1, 2, 0), pick(w_out, core)[None]], axis=0
    )
    attn_grid = spread_weights(attn_block)
    token_chunks = after(token_chunks, attn_grid[0])
    values = to_sequence(token_chunks, core).astype(jnp.float32)
    gains = jnp.stack([gain_attn, gain_ffn], axis=0)
    gains = jnp.concatenate([gains] + [hop(gains, "col", flip) for flip in range(1, 4)], axis=1)
    corner = [(4 * at + to, 4 * to + at) for at in range(4) for to in range(4)]
    segment_rows = lax.ppermute(segment_ids, ("row", "col"), corner)
    segment_rows = by_core(core, segment_rows, swap(segment_rows))
    segment = lax.dynamic_index_in_dim(segment_rows, col, 0, keepdims=False)
    ffn_block = jnp.concatenate(
        [pick(w_gate_up, core, 2).transpose(1, 2, 0), pick(w_down, core)[None]], axis=0
    )
    ffn_grid = spread_weights(ffn_block, attn_grid[0], attn_grid[1] + attn_grid[2])
    big_qkv, big_out = after(join_weights(attn_grid, (3, 1)), ffn_grid[0])
    grad_chunks = send_chunks(after(grad_out, ffn_grid[0]), core, col, length)
    big_gate_up, big_down = join_weights(ffn_grid, (2, 1))
    cotangent = to_sequence(after(grad_chunks, ffn_grid[1] + ffn_grid[2]), core)

    unit_one, rescale_one = norm_rows(values)
    normed_one = (unit_one * gains[0][None, :]).astype(jnp.bfloat16)
    packed = times_t(normed_one, big_qkv).astype(jnp.bfloat16)
    packed = packed.reshape(length, 3, heads, HEAD_DIM)
    queries, keys, vals = (packed[:, 0], packed[:, 1], packed[:, 2])
    scores = jnp.einsum("qhd,khd->hqk", queries, keys, preferred_element_type=jnp.float32) * factor
    spot = jnp.arange(length, dtype=jnp.int32)
    live = (segment[:, None] == segment[None, :]) & (spot[None, :] <= spot[:, None])
    scores = jnp.where(live[None], scores, MASKED)
    expo = jnp.exp(scores - jnp.max(scores, axis=-1, keepdims=True))
    prob = expo / jnp.sum(expo, axis=-1, keepdims=True)
    prob_low = prob.astype(jnp.bfloat16)
    mixed = jnp.einsum("hqk,khd->qhd", prob_low, vals, preferred_element_type=jnp.float32)
    mixed = mixed.reshape(length, -1).astype(jnp.bfloat16)
    branch = times(mixed, big_out)
    hidden_rows = values + (branch + swap(branch))
    unit_two, rescale_two = norm_rows(hidden_rows)
    normed_two = (unit_two * gains[1][None, :]).astype(jnp.bfloat16)
    gate_up = times_t(normed_two, big_gate_up).astype(jnp.bfloat16)
    half = gate_up.shape[1] // 2
    gate_vals = gate_up[:, :half].astype(jnp.float32)
    up_vals = gate_up[:, half:].astype(jnp.float32)
    sigmoid_gate = jax.nn.sigmoid(gate_vals)
    silu_gate = gate_vals * sigmoid_gate
    active = (silu_gate * up_vals).astype(jnp.bfloat16)

    down_state = start_cols(weight_grad(active, cotangent))
    grad_act = wide(low(times_t(cotangent, big_down)))
    grad_gate = grad_act * up_vals * sigmoid_gate * (1.0 + gate_vals * (1.0 - sigmoid_gate))
    grad_up = grad_act * silu_gate
    grad_gu = jnp.concatenate([grad_gate, grad_up], axis=1).astype(jnp.bfloat16)
    grad_two = times(grad_gu, big_gate_up)
    grad_two = grad_two + swap(grad_two)
    gate_up_state = start_rows(weight_grad(grad_gu, normed_two), 2)
    back_two = norm_rows_back(grad_two, unit_two, rescale_two, gains[1])
    gain_two = jnp.sum(pick(grad_two * unit_two, core), axis=0)
    grad_hidden = cotangent.astype(jnp.float32) + back_two
    grad_branch = grad_hidden.astype(jnp.bfloat16)
    grad_w_out = low(weight_grad(mixed, grad_branch))
    grad_mix = times_t(grad_branch, big_out).astype(jnp.bfloat16).reshape(length, heads, HEAD_DIM)
    grad_vals = jnp.einsum("hqk,qhd->khd", prob_low, grad_mix, preferred_element_type=jnp.float32)
    grad_prob = jnp.einsum("qhd,khd->hqk", grad_mix, vals, preferred_element_type=jnp.float32)
    inner = jnp.sum(prob * grad_prob, axis=-1, keepdims=True)
    grad_scores = (prob * (grad_prob - inner)).astype(jnp.bfloat16)
    grad_queries = factor * jnp.einsum(
        "hqk,khd->qhd", grad_scores, keys, preferred_element_type=jnp.float32
    )
    grad_keys = factor * jnp.einsum(
        "hqk,qhd->khd", grad_scores, queries, preferred_element_type=jnp.float32
    )
    grad_packed = jnp.stack([grad_queries, grad_keys, grad_vals], axis=1)
    grad_packed = grad_packed.astype(jnp.bfloat16).reshape(length, -1)
    grad_attn = jnp.concatenate([low(weight_grad(grad_packed, normed_one)), grad_w_out], axis=0)

    gate_up_sent, gate_up_state = middle_rows(after(gate_up_state, grad_attn))
    grad_attn = after(grad_attn, gate_up_sent)
    attn_state = start_rows(grad_attn, 4)
    down_sent, down_state = relay_last(after(down_state, grad_attn))
    active = after(active, grad_attn)
    grad_packed = after(grad_packed, grad_attn)
    grad_one = times(grad_packed, big_qkv)
    grad_one = pick(grad_one, core) + swap(pick(grad_one, 1 - core))
    ffn = times(active, big_down)
    ffn_mine = pick(ffn, core) + swap(pick(ffn, 1 - core))
    output = (pick(hidden_rows, core) + ffn_mine).astype(jnp.bfloat16)
    unit_mine = pick(unit_one, core)
    back_one = norm_rows_back(grad_one, unit_mine, pick(rescale_one, core), gains[0])
    gain_one = jnp.sum(grad_one * unit_mine, axis=0)
    grad_rows = (pick(grad_hidden, core) + back_one).astype(jnp.bfloat16)

    gate_up_state = after(gate_up_state, (output, grad_rows))
    parts = split_cols(end_rows(gate_up_state))
    gate_up_state = relay_cols(parts)
    output = send_rows(after(output, parts))
    down_rows = low(relay_sum(after(down_state, parts)))
    down_state = start_rows(down_rows, 1)
    attn_state = after(attn_state, down_rows)
    attn_sent, attn_state = middle_rows(attn_state)
    gate_up_state = after(gate_up_state, attn_sent)
    gate_up_sent, gate_up_state = relay_last(gate_up_state)
    down_sent, down_state = middle_rows(after(down_state, gate_up_sent))
    attn_state = after(attn_state, down_sent)
    attn_parts = split_cols(end_rows(attn_state))
    attn_got = send_cols(attn_parts)
    gain_sums = jnp.stack([gain_one, gain_two], axis=0)
    gain_sums, grad_rows = after((gain_sums, grad_rows), attn_parts)
    grad_tokens = from_sequence(send_rows(grad_rows), core, col, length).astype(jnp.float32)
    gate_up_state, down_state, output = after((gate_up_state, down_state, output), attn_parts)
    output = from_sequence(output, core, col, length)
    mine_gate_up = relay_sum(gate_up_state)
    mine_down = jnp.concatenate(end_rows(down_state), axis=-1)
    mine_attn = end_cols(attn_parts[0], attn_got)

    gain_sums = gain_sums + swap(gain_sums)
    gain_sums = gain_sums + hop(gain_sums, "row", 1)
    gain_sums = gain_sums + hop(gain_sums, "row", 2)
    gain_mine = gain_sums[:, :features]
    for flip in range(1, 4):
        piece = gain_sums[:, flip * features : (flip + 1) * features]
        gain_mine = gain_mine + hop(piece, "col", flip)

    whole_attn = joined(mine_attn, core)
    return (
        output,
        grad_tokens,
        gain_mine[0],
        gain_mine[1],
        whole_attn[:3].transpose(2, 0, 1),
        whole_attn[3],
        joined(mine_gate_up, core).transpose(2, 0, 1),
        joined(mine_down, core)[0],
    )


def layer(tokens, segment_ids, *rest):
    sizes = (lax.axis_size("dp"), lax.axis_size("row"), lax.axis_size("col"))
    if sizes == (2, 4, 4) and tokens.shape[0] == 2 * segment_ids.shape[1]:
        return chip_local(tokens, segment_ids, *rest)
    return local(tokens, segment_ids, *rest)


def solution(mesh):
    in_specs = (
        P(("dp", "row"), "col"),
        P(("dp", "col"), None),
        P("col"),
        P("col"),
        P("col", None, "row"),
        P("row", "col"),
        P("col", None, "row"),
        P("row", "col"),
        P(("dp", "row"), "col"),
    )
    out_specs = (
        P(("dp", "row"), "col"),
        P(("dp", "row"), "col"),
        P("col"),
        P("col"),
        P("col", None, "row"),
        P("row", "col"),
        P("col", None, "row"),
        P("row", "col"),
    )
    return jax.shard_map(layer, mesh=mesh, in_specs=in_specs, out_specs=out_specs, check_vma=False)
```

profile of v0, /device:TPU:0, one launch (start us, length us, event | category | flops | bytes accessed | tf_op | source)
XLA Modules:
  0.0 450.6 jit_solution(14770454800126176328)
XLA Ops:
  1.5 5.1 %collective-permute-start.38 = (f32[2,256]{1,0:T(2,128)S(1)}, f32[2,256]{1,0:T(2,128)S(1)}, u32[]{:S(2)}, u32[]{:S(2)}) collective-permute-start(f32[2,256]{1,0:T(2,128)S(1)} %pad_maximum_fusion.24), channel_id=1, source_target_pairs={{0,3},{1,2},{2,1},{3,0},{4,7},{5,6},{6,5},{7,4},{8,11},{9,10},{10,... | collective-permute-start | bytes 6152 | tf_op jit(solution)/shard_map/ppermute | solution.py:262
  17.3 8.6 %collective-permute-start.3 = (bf16[4,128,256]{2,1,0:T(8,128)(2,1)S(1)}, bf16[4,128,256]{2,1,0:T(8,128)(2,1)S(1)}, u32[]{:S(2)}, u32[]{:S(2)}) collective-permute-start(bf16[4,128,256]{2,1,0:T(8,128)(2,1)S(1)} %collective-permute-done.1.refs_1_), channel_id=1, source_target_pairs={{0,3},{1,2},{2,1},{3,0},{4,7},{5,6},{6,5},{7,4},{8,11},{9,10},{10,... | collective-permute-start | bytes 786440 | tf_op jit(solution)/shard_map/ppermute | solution.py:262
  26.3 10.2 %collective-permute-start.33 = (bf16[256,256]{1,0:T(8,128)(2,1)S(1)}, bf16[256,256]{1,0:T(8,128)(2,1)S(1)}, u32[]{:S(2)}, u32[]{:S(2)}) collective-permute-start(bf16[256,256]{1,0:T(8,128)(2,1)S(1)} %get-tuple-element.225), channel_id=1, source_target_pairs={{0,2},{1,3},{2,0},{3,1},{4,6},{5,7},{6,4},{7,5},{8,10},{9,11},{10,... | collective-permute-start | bytes 393224 | tf_op jit(solution)/shard_map/ppermute | solution.py:262
  39.6 8.6 %collective-permute-done.33 = bf16[256,256]{1,0:T(8,128)(2,1)S(1)} collective-permute-done((bf16[256,256]{1,0:T(8,128)(2,1)S(1)}, bf16[256,256]{1,0:T(8,128)(2,1)S(1)}, u32[]{:S(2)}, u32[]{:S(2)}) %collective-permute-start.33) | collective-permute-done | bytes 131104 | tf_op jit(solution)/shard_map/ppermute | solution.py:262
  58.9 4.1 collective-permute-done.6.refs_7_
  87.7 4.7 %shard_map.153 = (bf16[3,512,1024]{2,1,0:T(8,128)(2,1)}, bf16[1,512,1024]{2,1,0:T(8,128)(2,1)}) custom-call(bf16[4,128,256]{2,1,0:T(8,128)(2,1)} %copy-done.16, bf16[4,128,256]{2,1,0:T(8,128)(2,1)} %copy-done.32, bf16[4,128,256]{2,1,0:T(8,128)(2,1)} %copy-done.35, bf16[4,128,256]{2,1,0:T(8,128)(2,1)} %copy-done.33, bf16[4,128,256]{2,1,0:T(8,128)(2,1)} %copy-done.34, ...), custom_call_target="tpu_custom_call" | custom-call | tf_op jit(solution)/shard_map/pallas_call | solution.py:372
  99.6 8.3 %collective-permute-done.12.refs_2_ = bf16[3,352,256]{2,1,0:T(8,128)(2,1)S(1)} collective-permute-done((bf16[3,352,256]{2,1,0:T(8,128)(2,1)}, bf16[3,352,256]{2,1,0:T(8,128)(2,1)S(1)}, u32[]{:S(2)}, u32[]{:S(2)}) %collective-permute-start.12) | collective-permute-done | bytes 540704 | tf_op jit(solution)/shard_map/ppermute | solution.py:262
  114.7 5.5 %fusion.98 = (f32[8,512]{1,0:T(8,128)S(1)}, f32[8,512,512]{1,2,0:T(8,128)}) fusion(pred[512,512]{0,1:T(8,128)(4,1)S(1)} %copy-done.47, bf16[512,3,8,64]{0,3,2,1:T(8,128)(2,1)S(1)} %bitcast.244), kind=kOutput, calls=%fused_computation.248 | convolution fusion | flops 276824576 | bytes 9715712 | tf_op jit(solution)/shard_map/sub | solution.py:510
  120.3 4.4 fusion.29
  129.3 23.3 %collective-permute-start.15 = (bf16[256,256]{1,0:T(8,128)(2,1)S(1)}, bf16[256,256]{1,0:T(8,128)(2,1)S(1)}, u32[]{:S(2)}, u32[]{:S(2)}) collective-permute-start(bf16[256,256]{1,0:T(8,128)(2,1)S(1)} %get-tuple-element.228), channel_id=1, source_target_pairs={{0,1},{1,0},{2,3},{3,2},{4,5},{5,4},{6,7},{7,6},{8,9},{9,8},{10,11... | collective-permute-start | bytes 393224 | tf_op jit(solution)/shard_map/ppermute | solution.py:262
  152.6 11.3 %collective-permute-start.16 = (bf16[256,256]{1,0:T(8,128)(2,1)S(1)}, bf16[256,256]{1,0:T(8,128)(2,1)S(1)}, u32[]{:S(2)}, u32[]{:S(2)}) collective-permute-start(bf16[256,256]{1,0:T(8,128)(2,1)S(1)} %get-tuple-element.229), channel_id=1, source_target_pairs={{0,2},{1,3},{2,0},{3,1},{4,6},{5,7},{6,4},{7,5},{8,10},{9,11},{10,... | collective-permute-start | bytes 393224 | tf_op jit(solution)/shard_map/ppermute | solution.py:262
  165.7 5.2 %collective-permute-done.16 = bf16[256,256]{1,0:T(8,128)(2,1)S(1)} collective-permute-done((bf16[256,256]{1,0:T(8,128)(2,1)S(1)}, bf16[256,256]{1,0:T(8,128)(2,1)S(1)}, u32[]{:S(2)}, u32[]{:S(2)}) %collective-permute-start.16) | collective-permute-done | bytes 131104 | tf_op jit(solution)/shard_map/ppermute | solution.py:262
  177.1 10.2 %collective-permute-done.27.refs_12_ = bf16[3,352,256]{2,1,0:T(8,128)(2,1)S(1)} collective-permute-done((bf16[3,352,256]{2,1,0:T(8,128)(2,1)}, bf16[3,352,256]{2,1,0:T(8,128)(2,1)S(1)}, u32[]{:S(2)}, u32[]{:S(2)}) %collective-permute-start.27) | collective-permute-done | bytes 540704 | tf_op jit(solution)/shard_map/ppermute | solution.py:262
  187.2 11.0 %collective-permute-done.28.refs_13_ = bf16[3,352,256]{2,1,0:T(8,128)(2,1)S(1)} collective-permute-done((bf16[3,352,256]{2,1,0:T(8,128)(2,1)}, bf16[3,352,256]{2,1,0:T(8,128)(2,1)S(1)}, u32[]{:S(2)}, u32[]{:S(2)}) %collective-permute-start.28) | collective-permute-done | bytes 540704 | tf_op jit(solution)/shard_map/ppermute | solution.py:262
  199.9 8.1 %shard_map.152 = (bf16[2,1408,1024]{2,1,0:T(8,128)(2,1)}, bf16[1,1408,1024]{2,1,0:T(8,128)(2,1)}) custom-call(bf16[3,352,256]{2,1,0:T(8,128)(2,1)} %pad_maximum_fusion.9.refs_0_, bf16[3,352,256]{2,1,0:T(8,128)(2,1)} %collective-permute-done.11.refs_1_, bf16[3,352,256]{2,1,0:T(8,128)(2,1)} %copy-done.20, ...), custom_call_target="tpu_custom_call" | custom-call | tf_op jit(solution)/shard_map/pallas_call | solution.py:372
  222.3 3.7 convolution_convert_fusion
  262.1 4.1 collective-permute-done.46
  285.5 27.4 %collective-permute-start.57 = (bf16[1408,256]{1,0:T(8,128)(2,1)S(1)}, bf16[1408,256]{1,0:T(8,128)(2,1)S(1)}, u32[]{:S(2)}, u32[]{:S(2)}) collective-permute-start(bf16[1408,256]{1,0:T(8,128)(2,1)S(1)} %fusion.23), channel_id=1, source_target_pairs={{0,1},{1,0},{2,3},{3,2},{4,5},{5,4},{6,7},{7,6},{8,9},{9,8},{10,11... | collective-permute-start | bytes 2162696 | tf_op jit(solution)/shard_map/ppermute | solution.py:262
  317.2 11.8 %collective-permute-done.57 = bf16[1408,256]{1,0:T(8,128)(2,1)S(1)} collective-permute-done((bf16[1408,256]{1,0:T(8,128)(2,1)S(1)}, bf16[1408,256]{1,0:T(8,128)(2,1)S(1)}, u32[]{:S(2)}, u32[]{:S(2)}) %collective-permute-start.57) | collective-permute-done | bytes 720928 | tf_op jit(solution)/shard_map/ppermute | solution.py:262
  336.7 13.7 %collective-permute-done.53 = bf16[2,2,352,256]{3,2,1,0:T(8,128)(2,1)S(1)} collective-permute-done((bf16[2,2,352,256]{3,2,1,0:T(8,128)(2,1)S(1)}, bf16[2,2,352,256]{3,2,1,0:T(8,128)(2,1)S(1)}, u32[]{:S(2)}, u32[]{:S(2)}) %collective-permute-start.53) | collective-permute-done | bytes 720928 | tf_op jit(solution)/shard_map/ppermute | solution.py:262
  356.3 16.0 %collective-permute-start.63 = (bf16[256,256]{1,0:T(8,128)(2,1)S(1)}, bf16[256,256]{1,0:T(8,128)(2,1)S(1)}, u32[]{:S(2)}, u32[]{:S(2)}) collective-permute-start(bf16[256,256]{1,0:T(8,128)(2,1)S(1)} %get-tuple-element.220), channel_id=1, source_target_pairs={{0,1},{1,0},{2,3},{3,2},{4,5},{5,4},{6,7},{7,6},{8,9},{9,8},{10,11... | collective-permute-start | bytes 393224 | tf_op jit(solution)/shard_map/ppermute | solution.py:262
  382.1 5.3 %collective-permute-done.78 = f32[2,256]{1,0:T(2,128)S(1)} collective-permute-done((f32[2,256]{1,0:T(2,128)S(1)}, f32[2,256]{1,0:T(2,128)S(1)}, u32[]{:S(2)}, u32[]{:S(2)}) %collective-permute-start.78) | collective-permute-done | bytes 2080 | tf_op jit(solution)/shard_map/ppermute | solution.py:262
  396.4 10.7 %collective-permute-done.70 = bf16[256,256]{1,0:T(8,128)(2,1)S(1)} collective-permute-done((bf16[256,256]{1,0:T(8,128)(2,1)S(1)}, bf16[256,256]{1,0:T(8,128)(2,1)S(1)}, u32[]{:S(2)}, u32[]{:S(2)}) %collective-permute-start.70) | collective-permute-done | bytes 131104 | tf_op jit(solution)/shard_map/ppermute | solution.py:262
  412.8 14.0 %collective-permute-done.80 = bf16[4,128,256]{2,1,0:T(8,128)(2,1)S(1)} collective-permute-done((bf16[4,128,256]{2,1,0:T(8,128)(2,1)}, bf16[4,128,256]{2,1,0:T(8,128)(2,1)S(1)}, u32[]{:S(2)}, u32[]{:S(2)}) %collective-permute-start.80) | collective-permute-done | bytes 262176 | tf_op jit(solution)/shard_map/ppermute | solution.py:262
  (421 shorter events, 213.1 us)
Async XLA Ops:
  15.1 36.6 %collective-permute-start = (bf16[4,128,256]{2,1,0:T(8,128)(2,1)S(1)}, bf16[4,128,256]{2,1,0:T(8,128)(2,1)S(1)}, u32[]{:S(2)}, u32[]{:S(2)}) collective-permute-start(bf16[4,128,256]{2,1,0:T(8,128)(2,1)S(1)} %pad_maximum_fusion.17.refs_0_), channel_id=1, source_target_pairs={{0,4},{4,0},{8,12},{12,8},{1,5},{5,1},{9,13},{13,9},{2,6},{6,2},{1... | collective-permute-start | bytes 786440 | tf_op jit(solution)/shard_map/ppermute | solution.py:262
  17.3 32.4 %collective-permute-start.3 = (bf16[4,128,256]{2,1,0:T(8,128)(2,1)S(1)}, bf16[4,128,256]{2,1,0:T(8,128)(2,1)S(1)}, u32[]{:S(2)}, u32[]{:S(2)}) collective-permute-start(bf16[4,128,256]{2,1,0:T(8,128)(2,1)S(1)} %collective-permute-done.1.refs_1_), channel_id=1, source_target_pairs={{0,3},{1,2},{2,1},{3,0},{4,7},{5,6},{6,5},{7,4},{8,11},{9,10},{10,... | collective-permute-start | bytes 786440 | tf_op jit(solution)/shard_map/ppermute | solution.py:262
  64.4 28.0 %collective-permute-start.11 = (bf16[3,352,256]{2,1,0:T(8,128)(2,1)}, bf16[3,352,256]{2,1,0:T(8,128)(2,1)}, u32[]{:S(2)}, u32[]{:S(2)}) collective-permute-start(bf16[3,352,256]{2,1,0:T(8,128)(2,1)} %pad_maximum_fusion.9.refs_0_), channel_id=1, source_target_pairs={{0,1},{1,0},{2,3},{3,2},{4,5},{5,4},{6,7},{7,6},{8,9},{9,8},{10,11... | collective-permute-start | bytes 1622024 | tf_op jit(solution)/shard_map/ppermute | solution.py:262
  67.6 25.8 %collective-permute-start.35 = (bf16[256,1024]{1,0:T(8,128)(2,1)S(1)}, bf16[256,1024]{1,0:T(8,128)(2,1)S(1)}, u32[]{:S(2)}, u32[]{:S(2)}) collective-permute-start(bf16[256,1024]{1,0:T(8,128)(2,1)S(1)} %constant_dynamic-update-slice_fusion.4), channel_id=1, source_target_pairs={{0,16},{16,0},{1,17},{17,1},{2,18},{18,2},{3,19},{19,3},{4,20},{20... | collective-permute-start | bytes 1572872 | tf_op jit(solution)/shard_map/ppermute | solution.py:258
  83.7 41.0 %collective-permute-start.18 = (bf16[3,352,256]{2,1,0:T(8,128)(2,1)}, bf16[3,352,256]{2,1,0:T(8,128)(2,1)}, u32[]{:S(2)}, u32[]{:S(2)}) collective-permute-start(bf16[3,352,256]{2,1,0:T(8,128)(2,1)} %pad_maximum_fusion.9.refs_0_), channel_id=1, source_target_pairs={{0,4},{4,0},{8,12},{12,8},{1,5},{5,1},{9,13},{13,9},{2,6},{6,2},{1... | collective-permute-start | bytes 1622024 | tf_op jit(solution)/shard_map/ppermute | solution.py:262
  86.0 40.2 %collective-permute-start.22 = (bf16[3,352,256]{2,1,0:T(8,128)(2,1)}, bf16[3,352,256]{2,1,0:T(8,128)(2,1)}, u32[]{:S(2)}, u32[]{:S(2)}) collective-permute-start(bf16[3,352,256]{2,1,0:T(8,128)(2,1)} %pad_maximum_fusion.9.refs_0_), channel_id=1, source_target_pairs={{0,8},{4,12},{8,0},{12,4},{1,9},{5,13},{9,1},{13,5},{2,10},{6,14},... | collective-permute-start | bytes 1622024 | tf_op jit(solution)/shard_map/ppermute | solution.py:262
  93.8 33.1 %collective-permute-start.19 = (bf16[3,352,256]{2,1,0:T(8,128)(2,1)}, bf16[3,352,256]{2,1,0:T(8,128)(2,1)}, u32[]{:S(2)}, u32[]{:S(2)}) collective-permute-start(bf16[3,352,256]{2,1,0:T(8,128)(2,1)} %collective-permute-done.11.refs_1_), channel_id=1, source_target_pairs={{0,4},{4,0},{8,12},{12,8},{1,5},{5,1},{9,13},{13,9},{2,6},{6,2},{1... | collective-permute-start | bytes 1622024 | tf_op jit(solution)/shard_map/ppermute | solution.py:262
  97.4 31.9 %collective-permute-start.23 = (bf16[3,352,256]{2,1,0:T(8,128)(2,1)}, bf16[3,352,256]{2,1,0:T(8,128)(2,1)}, u32[]{:S(2)}, u32[]{:S(2)}) collective-permute-start(bf16[3,352,256]{2,1,0:T(8,128)(2,1)} %collective-permute-done.11.refs_1_), channel_id=1, source_target_pairs={{0,8},{4,12},{8,0},{12,4},{1,9},{5,13},{9,1},{13,5},{2,10},{6,14},... | collective-permute-start | bytes 1622024 | tf_op jit(solution)/shard_map/ppermute | solution.py:262
  124.7 27.9 %collective-permute-start.25 = (bf16[3,352,256]{2,1,0:T(8,128)(2,1)}, bf16[3,352,256]{2,1,0:T(8,128)(2,1)S(1)}, u32[]{:S(2)}, u32[]{:S(2)}) collective-permute-start(bf16[3,352,256]{2,1,0:T(8,128)(2,1)} %collective-permute-done.13.refs_3_), channel_id=1, source_target_pairs={{0,8},{4,12},{8,0},{12,4},{1,9},{5,13},{9,1},{13,5},{2,10},{6,14},... | collective-permute-start | bytes 1622024 | tf_op jit(solution)/shard_map/ppermute | solution.py:262
  126.9 81.2 %collective-permute-start.45 = (f32[512,1024]{1,0:T(8,128)S(1)}, f32[512,1024]{1,0:T(8,128)}, u32[]{:S(2)}, u32[]{:S(2)}) collective-permute-start(f32[512,1024]{1,0:T(8,128)S(1)} %fusion.99), channel_id=1, source_target_pairs={{0,16},{16,0},{1,17},{17,1},{2,18},{18,2},{3,19},{19,3},{4,20},{20... | collective-permute-start | bytes 6291464 | tf_op jit(solution)/shard_map/ppermute | solution.py:258
  127.4 43.4 %collective-permute-start.20 = (bf16[3,352,256]{2,1,0:T(8,128)(2,1)S(1)}, bf16[3,352,256]{2,1,0:T(8,128)(2,1)S(1)}, u32[]{:S(2)}, u32[]{:S(2)}) collective-permute-start(bf16[3,352,256]{2,1,0:T(8,128)(2,1)S(1)} %copy-done.21), channel_id=1, source_target_pairs={{0,4},{4,0},{8,12},{12,8},{1,5},{5,1},{9,13},{13,9},{2,6},{6,2},{1... | collective-permute-start | bytes 1622024 | tf_op jit(solution)/shard_map/ppermute | solution.py:262
  128.2 42.6 %collective-permute-start.24 = (bf16[3,352,256]{2,1,0:T(8,128)(2,1)S(1)}, bf16[3,352,256]{2,1,0:T(8,128)(2,1)S(1)}, u32[]{:S(2)}, u32[]{:S(2)}) collective-permute-start(bf16[3,352,256]{2,1,0:T(8,128)(2,1)S(1)} %copy-done.21), channel_id=1, source_target_pairs={{0,8},{4,12},{8,0},{12,4},{1,9},{5,13},{9,1},{13,5},{2,10},{6,14},... | collective-permute-start | bytes 1622024 | tf_op jit(solution)/shard_map/ppermute | solution.py:262
  129.3 34.6 %collective-permute-start.15 = (bf16[256,256]{1,0:T(8,128)(2,1)S(1)}, bf16[256,256]{1,0:T(8,128)(2,1)S(1)}, u32[]{:S(2)}, u32[]{:S(2)}) collective-permute-start(bf16[256,256]{1,0:T(8,128)(2,1)S(1)} %get-tuple-element.228), channel_id=1, source_target_pairs={{0,1},{1,0},{2,3},{3,2},{4,5},{5,4},{6,7},{7,6},{8,9},{9,8},{10,11... | collective-permute-start | bytes 393224 | tf_op jit(solution)/shard_map/ppermute | solution.py:262
  173.4 24.9 %collective-permute-start.28 = (bf16[3,352,256]{2,1,0:T(8,128)(2,1)}, bf16[3,352,256]{2,1,0:T(8,128)(2,1)S(1)}, u32[]{:S(2)}, u32[]{:S(2)}) collective-permute-start(bf16[3,352,256]{2,1,0:T(8,128)(2,1)} %collective-permute-done.19.refs_5_), channel_id=1, source_target_pairs={{0,8},{4,12},{8,0},{12,4},{1,9},{5,13},{9,1},{13,5},{2,10},{6,14},... | collective-permute-start | bytes 1622024 | tf_op jit(solution)/shard_map/ppermute | solution.py:262
  231.9 34.3 %collective-permute-start.46 = (bf16[2,2,352,512]{3,2,0,1:T(8,128)(2,1)}, bf16[2,2,352,512]{3,2,0,1:T(8,128)(2,1)}, u32[]{:S(2)}, u32[]{:S(2)}) collective-permute-start(bf16[2,2,352,512]{3,2,0,1:T(8,128)(2,1)} %copy_bitcast_fusion.1), channel_id=1, source_target_pairs={{0,8},{4,12},{8,0},{12,4},{1,9},{5,13},{9,1},{13,5},{2,10},{6,14},... | collective-permute-start | bytes 4325384 | tf_op jit(solution)/shard_map/ppermute | solution.py:262
  234.7 34.0 %collective-permute-start.47 = (bf16[2,2,352,512]{3,2,0,1:T(8,128)(2,1)}, bf16[2,2,352,512]{3,2,0,1:T(8,128)(2,1)}, u32[]{:S(2)}, u32[]{:S(2)}) collective-permute-start(bf16[2,2,352,512]{3,2,0,1:T(8,128)(2,1)} %copy_bitcast_fusion), channel_id=1, source_target_pairs={{0,4},{4,0},{8,12},{12,8},{1,5},{5,1},{9,13},{13,9},{2,6},{6,2},{1... | collective-permute-start | bytes 4325384 | tf_op jit(solution)/shard_map/ppermute | solution.py:262
  239.9 38.8 %collective-permute-start.56 = (bf16[2,1408,256]{2,1,0:T(8,128)(2,1)}, bf16[2,1408,256]{2,1,0:T(8,128)(2,1)}, u32[]{:S(2)}, u32[]{:S(2)}) collective-permute-start(bf16[2,1408,256]{2,1,0:T(8,128)(2,1)} %pad_maximum_fusion.5), channel_id=1, source_target_pairs={{0,3},{1,2},{2,1},{3,0},{4,7},{5,6},{6,5},{7,4},{8,11},{9,10},{10,... | collective-permute-start | bytes 4325384 | tf_op jit(solution)/shard_map/ppermute | solution.py:262
  270.1 43.5 %collective-permute-start.49 = (bf16[2,352,512]{2,1,0:T(8,128)(2,1)S(1)}, bf16[2,352,512]{2,1,0:T(8,128)(2,1)S(1)}, u32[]{:S(2)}, u32[]{:S(2)}) collective-permute-start(bf16[2,352,512]{2,1,0:T(8,128)(2,1)S(1)} %fusion.28), channel_id=1, source_target_pairs={{0,4},{4,0},{8,12},{12,8},{1,5},{5,1},{9,13},{13,9},{2,6},{6,2},{1... | collective-permute-start | bytes 2162696 | tf_op jit(solution)/shard_map/ppermute | solution.py:262
  273.4 40.1 %collective-permute-start.50 = (bf16[2,352,512]{2,1,0:T(8,128)(2,1)}, bf16[2,352,512]{2,1,0:T(8,128)(2,1)}, u32[]{:S(2)}, u32[]{:S(2)}) collective-permute-start(bf16[2,352,512]{2,1,0:T(8,128)(2,1)} %fusion.27), channel_id=1, source_target_pairs={{0,8},{4,12},{8,0},{12,4},{1,9},{5,13},{9,1},{13,5},{2,10},{6,14},... | collective-permute-start | bytes 2162696 | tf_op jit(solution)/shard_map/ppermute | solution.py:262
  277.1 52.1 %collective-permute-start.54 = (bf16[4,2,128,512]{3,2,0,1:T(8,128)(2,1)S(1)}, bf16[4,2,128,512]{3,2,0,1:T(8,128)(2,1)S(1)}, u32[]{:S(2)}, u32[]{:S(2)}) collective-permute-start(bf16[4,2,128,512]{3,2,0,1:T(8,128)(2,1)S(1)} %copy_bitcast_fusion.3), channel_id=1, source_target_pairs={{0,8},{4,12},{8,0},{12,4},{1,9},{5,13},{9,1},{13,5},{2,10},{6,14},... | collective-permute-start | bytes 3145736 | tf_op jit(solution)/shard_map/ppermute | solution.py:262
  284.3 44.9 %collective-permute-start.55 = (bf16[4,2,128,512]{3,2,0,1:T(8,128)(2,1)S(1)}, bf16[4,2,128,512]{3,2,0,1:T(8,128)(2,1)S(1)}, u32[]{:S(2)}, u32[]{:S(2)}) collective-permute-start(bf16[4,2,128,512]{3,2,0,1:T(8,128)(2,1)S(1)} %copy_bitcast_fusion.2), channel_id=1, source_target_pairs={{0,4},{4,0},{8,12},{12,8},{1,5},{5,1},{9,13},{13,9},{2,6},{6,2},{1... | collective-permute-start | bytes 3145736 | tf_op jit(solution)/shard_map/ppermute | solution.py:262
  285.5 43.5 %collective-permute-start.57 = (bf16[1408,256]{1,0:T(8,128)(2,1)S(1)}, bf16[1408,256]{1,0:T(8,128)(2,1)S(1)}, u32[]{:S(2)}, u32[]{:S(2)}) collective-permute-start(bf16[1408,256]{1,0:T(8,128)(2,1)S(1)} %fusion.23), channel_id=1, source_target_pairs={{0,1},{1,0},{2,3},{3,2},{4,5},{5,4},{6,7},{7,6},{8,9},{9,8},{10,11... | collective-permute-start | bytes 2162696 | tf_op jit(solution)/shard_map/ppermute | solution.py:262
  356.3 54.2 %collective-permute-start.63 = (bf16[256,256]{1,0:T(8,128)(2,1)S(1)}, bf16[256,256]{1,0:T(8,128)(2,1)S(1)}, u32[]{:S(2)}, u32[]{:S(2)}) collective-permute-start(bf16[256,256]{1,0:T(8,128)(2,1)S(1)} %get-tuple-element.220), channel_id=1, source_target_pairs={{0,1},{1,0},{2,3},{3,2},{4,5},{5,4},{6,7},{7,6},{8,9},{9,8},{10,11... | collective-permute-start | bytes 393224 | tf_op jit(solution)/shard_map/ppermute | solution.py:262
  374.7 57.3 %collective-permute-start.58 = (bf16[2,352,256]{2,1,0:T(8,128)(2,1)}, bf16[2,352,256]{2,1,0:T(8,128)(2,1)S(1)}, u32[]{:S(2)}, u32[]{:S(2)}) collective-permute-start(bf16[2,352,256]{2,1,0:T(8,128)(2,1)} %fusion.51), channel_id=1, source_target_pairs={{0,1},{1,0},{2,3},{3,2},{4,5},{5,4},{6,7},{7,6},{8,9},{9,8},{10,11... | collective-permute-start | bytes 1081352 | tf_op jit(solution)/shard_map/ppermute | solution.py:262
  (131 other events, 1608.8 us)
where the time goes:
time: 456 us; the launch traced here: 451 us
  starting transfers between devices  188 us (41%)
  waiting for transfers between devices  130 us (29%)
  matrix products  45.4 us (10%)
  other arithmetic  33.8 us (7%)
  local copies, waits for them, and re-layouts  31.6 us (7%)
  Pallas kernels  19.3 us (4%)
    ppermute x69, starting transfers between devices, hop(): lax.ppermute(values, axis, [(at, at ^ flip) for at in range(lax.axis_size...  185 us
    ppermute x69, waiting for transfers between devices, hop(): lax.ppermute(values, axis, [(at, at ^ flip) for at in range(lax.axis_size...  129 us
    pallas_call x2, Pallas kernels, join_weights(): pl.pallas_call(join_blocks, out_shape=shapes)  12.8 us
    dot_general x4, matrix products, times_t(): lax.dot_general(left, right, (((1,), (1,)), ((), ())), preferred_element_...  10.9 us
    unnamed x146, local copies, waits for them, and re-layouts  10.2 us
    convert_element_type x12, other arithmetic, low(): return values.astype(jnp.bfloat16)  9.68 us
  transfers between devices with their start and end apart: 85, of which 23 were waited for; matrix products, arithmetic and copies ran while one was open for 18% of the time, Pallas kernels for 4%

commit v1 on v0

--- a/solution.py
+++ b/solution.py
@@ -404,23 +404,6 @@
     return (sums, sums_r)
 
 
-def relay_cols(parts):
-    own, first, second, third = parts
-    got = hop(jnp.stack([third, second]), "col", 3)
-    return (own, first, got)
-
-
-def relay_last(state):
-    own, first, got = state
-    sent = low(wide(first) + wide(got[1]))
-    return (sent, (own, got[0], hop(sent, "col", 1)))
-
-
-def relay_sum(state):
-    own, got, last = state
-    return wide(own) + wide(got) + wide(last)
-
-
 def split_cols(state):
     sums, sums_r = state
     width = sums.shape[-1] // 2
@@ -438,7 +421,8 @@
 
 def start_cols(grad):
     width = grad.shape[1] // 4
-    return relay_cols([low(grad[:, at * width : (at + 1) * width]) for at in range(4)])
+    parts = [low(grad[:, at * width : (at + 1) * width]) for at in range(4)]
+    return parts[:1] + send_cols(parts)
 
 
 def join_halves(core_ref, mine, other, whole):
@@ -494,9 +478,10 @@
     )
     ffn_grid = spread_weights(ffn_block, attn_grid[0], attn_grid[1] + attn_grid[2])
     big_qkv, big_out = after(join_weights(attn_grid, (3, 1)), ffn_grid[0])
-    grad_chunks = send_chunks(after(grad_out, ffn_grid[0]), core, col, length)
+    grad_late = after(grad_out, ffn_grid[1] + ffn_grid[2])
+    grad_chunks = send_chunks(grad_late, core, col, length)
     big_gate_up, big_down = join_weights(ffn_grid, (2, 1))
-    cotangent = to_sequence(after(grad_chunks, ffn_grid[1] + ffn_grid[2]), core)
+    cotangent = to_sequence(grad_chunks, core)
 
     unit_one, rescale_one = norm_rows(values)
     normed_one = (unit_one * gains[0][None, :]).astype(jnp.bfloat16)
@@ -555,7 +540,6 @@
     gate_up_sent, gate_up_state = middle_rows(after(gate_up_state, grad_attn))
     grad_attn = after(grad_attn, gate_up_sent)
     attn_state = start_rows(grad_attn, 4)
-    down_sent, down_state = relay_last(after(down_state, grad_attn))
     active = after(active, grad_attn)
     grad_packed = after(grad_packed, grad_attn)
     grad_one = times(grad_packed, big_qkv)
@@ -570,24 +554,22 @@
 
     gate_up_state = after(gate_up_state, (output, grad_rows))
     parts = split_cols(end_rows(gate_up_state))
-    gate_up_state = relay_cols(parts)
+    gate_up_got = send_cols(parts)
     output = send_rows(after(output, parts))
-    down_rows = low(relay_sum(after(down_state, parts)))
+    down_state = after(down_state, parts)
+    down_rows = low(end_cols(wide(down_state[0]), down_state[1:]))
     down_state = start_rows(down_rows, 1)
-    attn_state = after(attn_state, down_rows)
-    attn_sent, attn_state = middle_rows(attn_state)
-    gate_up_state = after(gate_up_state, attn_sent)
-    gate_up_sent, gate_up_state = relay_last(gate_up_state)
-    down_sent, down_state = middle_rows(after(down_state, gate_up_sent))
+    attn_sent, attn_state = middle_rows(after(attn_state, down_rows))
+    down_sent, down_state = middle_rows(after(down_state, attn_sent))
     attn_state = after(attn_state, down_sent)
     attn_parts = split_cols(end_rows(attn_state))
     attn_got = send_cols(attn_parts)
     gain_sums = jnp.stack([gain_one, gain_two], axis=0)
     gain_sums, grad_rows = after((gain_sums, grad_rows), attn_parts)
     grad_tokens = from_sequence(send_rows(grad_rows), core, col, length).astype(jnp.float32)
-    gate_up_state, down_state, output = after((gate_up_state, down_state, output), attn_parts)
+    gate_up_got, down_state, output = after((gate_up_got, down_state, output), attn_parts)
     output = from_sequence(output, core, col, length)
-    mine_gate_up = relay_sum(gate_up_state)
+    mine_gate_up = end_cols(parts[0], gate_up_got)
     mine_down = jnp.concatenate(end_rows(down_state), axis=-1)
     mine_attn = end_cols(attn_parts[0], attn_got)
 

time: 456 us -> 461 us (1.011)
  waiting for transfers between devices: 130 us -> 188 us
  starting transfers between devices: 188 us -> 138 us
    ppermute x69 -> x71, waiting for transfers between devices: 129 us -> 186 us  [hop(): lax.ppermute(values, axis, [(at, at ^ flip) for at in range(lax.axis_size...]
    ppermute x69 -> x71, starting transfers between devices: 185 us -> 136 us  [hop(): lax.ppermute(values, axis, [(at, at ^ flip) for at in range(lax.axis_size...]
    unnamed x146 -> x119, local copies, waits for them, and re-layouts: 10.2 us -> 9.96 us
    convert_element_type x12 -> x10, other arithmetic: 9.68 us -> 9.53 us  [low(): return values.astype(jnp.bfloat16)]
  transfers between devices with their start and end apart: 85 -> 87, of which waited for: 23 -> 32; matrix products, arithmetic and copies ran while one was open for 18% -> 18% of each run, Pallas kernels for 4% -> 4%
where the time goes in v1:
time: 461 us; the launch traced here: 455 us
  waiting for transfers between devices  188 us (41%)
  starting transfers between devices  138 us (30%)
  matrix products  45.4 us (10%)
  other arithmetic  32 us (7%)
  local copies, waits for them, and re-layouts  30.4 us (7%)
  Pallas kernels  19.4 us (4%)
    ppermute x71, waiting for transfers between devices, hop(): lax.ppermute(values, axis, [(at, at ^ flip) for at in range(lax.axis_size...  186 us
    ppermute x71, starting transfers between devices, hop(): lax.ppermute(values, axis, [(at, at ^ flip) for at in range(lax.axis_size...  136 us
    pallas_call x2, Pallas kernels, join_weights(): pl.pallas_call(join_blocks, out_shape=shapes)  12.8 us
    dot_general x4, matrix products, times_t(): lax.dot_general(left, right, (((1,), (1,)), ((), ())), preferred_element_...  10.9 us
    unnamed x119, local copies, waits for them, and re-layouts  9.96 us
    convert_element_type x10, other arithmetic, low(): return values.astype(jnp.bfloat16)  9.53 us
  transfers between devices with their start and end apart: 87, of which 32 were waited for; matrix products, arithmetic and copies ran while one was open for 18% of the time, Pallas kernels for 4%

profile of v1, /device:TPU:0, one launch (start us, length us, event | category | flops | bytes accessed | tf_op | source)
XLA Modules:
  0.0 455.1 jit_solution(9681741298847396908)
XLA Ops:
  1.5 5.1 %collective-permute-start.38 = (f32[2,256]{1,0:T(2,128)S(1)}, f32[2,256]{1,0:T(2,128)S(1)}, u32[]{:S(2)}, u32[]{:S(2)}) collective-permute-start(f32[2,256]{1,0:T(2,128)S(1)} %pad_maximum_fusion.23), channel_id=1, source_target_pairs={{0,3},{1,2},{2,1},{3,0},{4,7},{5,6},{6,5},{7,4},{8,11},{9,10},{10,... | collective-permute-start | bytes 6152 | tf_op jit(solution)/shard_map/ppermute | solution.py:262
  17.3 8.6 %collective-permute-start.3 = (bf16[4,128,256]{2,1,0:T(8,128)(2,1)S(1)}, bf16[4,128,256]{2,1,0:T(8,128)(2,1)S(1)}, u32[]{:S(2)}, u32[]{:S(2)}) collective-permute-start(bf16[4,128,256]{2,1,0:T(8,128)(2,1)S(1)} %collective-permute-done.1.refs_1_), channel_id=1, source_target_pairs={{0,3},{1,2},{2,1},{3,0},{4,7},{5,6},{6,5},{7,4},{8,11},{9,10},{10,... | collective-permute-start | bytes 786440 | tf_op jit(solution)/shard_map/ppermute | solution.py:262
  26.3 10.2 %collective-permute-start.33 = (bf16[256,256]{1,0:T(8,128)(2,1)S(1)}, bf16[256,256]{1,0:T(8,128)(2,1)S(1)}, u32[]{:S(2)}, u32[]{:S(2)}) collective-permute-start(bf16[256,256]{1,0:T(8,128)(2,1)S(1)} %get-tuple-element.207), channel_id=1, source_target_pairs={{0,2},{1,3},{2,0},{3,1},{4,6},{5,7},{6,4},{7,5},{8,10},{9,11},{10,... | collective-permute-start | bytes 393224 | tf_op jit(solution)/shard_map/ppermute | solution.py:262
  39.6 8.6 %collective-permute-done.33 = bf16[256,256]{1,0:T(8,128)(2,1)S(1)} collective-permute-done((bf16[256,256]{1,0:T(8,128)(2,1)S(1)}, bf16[256,256]{1,0:T(8,128)(2,1)S(1)}, u32[]{:S(2)}, u32[]{:S(2)}) %collective-permute-start.33) | collective-permute-done | bytes 131104 | tf_op jit(solution)/shard_map/ppermute | solution.py:262
  58.9 4.1 collective-permute-done.6.refs_7_
  87.7 4.7 %shard_map.153 = (bf16[3,512,1024]{2,1,0:T(8,128)(2,1)}, bf16[1,512,1024]{2,1,0:T(8,128)(2,1)}) custom-call(bf16[4,128,256]{2,1,0:T(8,128)(2,1)} %copy-done.12, bf16[4,128,256]{2,1,0:T(8,128)(2,1)} %copy-done.26, bf16[4,128,256]{2,1,0:T(8,128)(2,1)} %copy-done.29, bf16[4,128,256]{2,1,0:T(8,128)(2,1)} %copy-done.27, bf16[4,128,256]{2,1,0:T(8,128)(2,1)} %copy-done.28, ...), custom_call_target="tpu_custom_call" | custom-call | tf_op jit(solution)/shard_map/pallas_call | solution.py:372
  99.6 8.3 %collective-permute-done.14.refs_2_ = bf16[3,352,256]{2,1,0:T(8,128)(2,1)S(1)} collective-permute-done((bf16[3,352,256]{2,1,0:T(8,128)(2,1)}, bf16[3,352,256]{2,1,0:T(8,128)(2,1)S(1)}, u32[]{:S(2)}, u32[]{:S(2)}) %collective-permute-start.14) | collective-permute-done | bytes 540704 | tf_op jit(solution)/shard_map/ppermute | solution.py:262
  114.7 5.5 %fusion.98 = (f32[8,512]{1,0:T(8,128)S(1)}, f32[8,512,512]{1,2,0:T(8,128)}) fusion(pred[512,512]{0,1:T(8,128)(4,1)S(1)} %copy-done.41, bf16[512,3,8,64]{0,3,2,1:T(8,128)(2,1)S(1)} %bitcast.226), kind=kOutput, calls=%fused_computation.235 | convolution fusion | flops 276824576 | bytes 9715712 | tf_op jit(solution)/shard_map/sub | solution.py:495
  120.3 4.4 fusion.28
  128.4 11.8 %collective-permute-done.21.refs_11_ = bf16[3,352,256]{2,1,0:T(8,128)(2,1)} collective-permute-done((bf16[3,352,256]{2,1,0:T(8,128)(2,1)}, bf16[3,352,256]{2,1,0:T(8,128)(2,1)}, u32[]{:S(2)}, u32[]{:S(2)}) %collective-permute-start.21) | collective-permute-done | bytes 540704 | tf_op jit(solution)/shard_map/ppermute | solution.py:262
  140.2 8.8 %collective-permute-done.20.refs_10_ = bf16[3,352,256]{2,1,0:T(8,128)(2,1)} collective-permute-done((bf16[3,352,256]{2,1,0:T(8,128)(2,1)S(1)}, bf16[3,352,256]{2,1,0:T(8,128)(2,1)}, u32[]{:S(2)}, u32[]{:S(2)}) %collective-permute-start.20) | collective-permute-done | bytes 540704 | tf_op jit(solution)/shard_map/ppermute | solution.py:262
  153.8 23.2 %collective-permute-start.24 = (bf16[256,256]{1,0:T(8,128)(2,1)S(1)}, bf16[256,256]{1,0:T(8,128)(2,1)S(1)}, u32[]{:S(2)}, u32[]{:S(2)}) collective-permute-start(bf16[256,256]{1,0:T(8,128)(2,1)S(1)} %get-tuple-element.210), channel_id=1, source_target_pairs={{0,2},{1,3},{2,0},{3,1},{4,6},{5,7},{6,4},{7,5},{8,10},{9,11},{10,... | collective-permute-start | bytes 393224 | tf_op jit(solution)/shard_map/ppermute | solution.py:262
  178.3 7.8 %collective-permute-done.24 = bf16[256,256]{1,0:T(8,128)(2,1)S(1)} collective-permute-done((bf16[256,256]{1,0:T(8,128)(2,1)S(1)}, bf16[256,256]{1,0:T(8,128)(2,1)S(1)}, u32[]{:S(2)}, u32[]{:S(2)}) %collective-permute-start.24) | collective-permute-done | bytes 131104 | tf_op jit(solution)/shard_map/ppermute | solution.py:262
  191.0 10.5 %collective-permute-done.30.refs_15_ = bf16[3,352,256]{2,1,0:T(8,128)(2,1)} collective-permute-done((bf16[3,352,256]{2,1,0:T(8,128)(2,1)}, bf16[3,352,256]{2,1,0:T(8,128)(2,1)}, u32[]{:S(2)}, u32[]{:S(2)}) %collective-permute-start.30) | collective-permute-done | bytes 540704 | tf_op jit(solution)/shard_map/ppermute | solution.py:262
  201.5 9.9 %collective-permute-done.29.refs_14_ = bf16[3,352,256]{2,1,0:T(8,128)(2,1)} collective-permute-done((bf16[3,352,256]{2,1,0:T(8,128)(2,1)}, bf16[3,352,256]{2,1,0:T(8,128)(2,1)}, u32[]{:S(2)}, u32[]{:S(2)}) %collective-permute-start.29) | collective-permute-done | bytes 540704 | tf_op jit(solution)/shard_map/ppermute | solution.py:262
  211.4 8.1 %shard_map.152 = (bf16[2,1408,1024]{2,1,0:T(8,128)(2,1)}, bf16[1,1408,1024]{2,1,0:T(8,128)(2,1)}) custom-call(bf16[3,352,256]{2,1,0:T(8,128)(2,1)} %pad_maximum_fusion.7.refs_0_, bf16[3,352,256]{2,1,0:T(8,128)(2,1)} %collective-permute-done.12.refs_1_, bf16[3,352,256]{2,1,0:T(8,128)(2,1)} %copy-done.17, ...), custom_call_target="tpu_custom_call" | custom-call | tf_op jit(solution)/shard_map/pallas_call | solution.py:372
  273.7 5.4 %collective-permute-done.46 = bf16[2,2,352,512]{3,2,0,1:T(8,128)(2,1)} collective-permute-done((bf16[2,2,352,512]{3,2,0,1:T(8,128)(2,1)}, bf16[2,2,352,512]{3,2,0,1:T(8,128)(2,1)}, u32[]{:S(2)}, u32[]{:S(2)}) %collective-permute-start.46) | collective-permute-done | bytes 1441824 | tf_op jit(solution)/shard_map/ppermute | solution.py:262
  301.9 12.7 %collective-permute-done.50 = bf16[2,352,512]{2,1,0:T(8,128)(2,1)S(1)} collective-permute-done((bf16[2,352,512]{2,1,0:T(8,128)(2,1)S(1)}, bf16[2,352,512]{2,1,0:T(8,128)(2,1)S(1)}, u32[]{:S(2)}, u32[]{:S(2)}) %collective-permute-start.50) | collective-permute-done | bytes 720928 | tf_op jit(solution)/shard_map/ppermute | solution.py:262
  320.5 16.1 %collective-permute-done.61 = bf16[4,2,128,512]{3,2,0,1:T(8,128)(2,1)S(1)} collective-permute-done((bf16[4,2,128,512]{3,2,0,1:T(8,128)(2,1)S(1)}, bf16[4,2,128,512]{3,2,0,1:T(8,128)(2,1)S(1)}, u32[]{:S(2)}, u32[]{:S(2)}) %collective-permute-start.61) | collective-permute-done | bytes 1048608 | tf_op jit(solution)/shard_map/ppermute | solution.py:262
  343.4 12.6 %collective-permute-done.59 = bf16[1,2,352,128]{3,2,1,0:T(8,128)(2,1)S(1)} collective-permute-done((bf16[1,2,352,128]{3,2,1,0:T(8,128)(2,1)S(1)}, bf16[1,2,352,128]{3,2,1,0:T(8,128)(2,1)S(1)}, u32[]{:S(2)}, u32[]{:S(2)}) %collective-permute-start.59) | collective-permute-done | bytes 180256 | tf_op jit(solution)/shard_map/ppermute | solution.py:262
  361.9 12.7 %collective-permute-done.65 = bf16[256,256]{1,0:T(8,128)(2,1)S(1)} collective-permute-done((bf16[256,256]{1,0:T(8,128)(2,1)S(1)}, bf16[256,256]{1,0:T(8,128)(2,1)S(1)}, u32[]{:S(2)}, u32[]{:S(2)}) %collective-permute-start.65) | collective-permute-done | bytes 131104 | tf_op jit(solution)/shard_map/ppermute | solution.py:262
  377.0 18.0 %collective-permute-done.66 = bf16[256,256]{1,0:T(8,128)(2,1)S(1)} collective-permute-done((bf16[256,256]{1,0:T(8,128)(2,1)S(1)}, bf16[256,256]{1,0:T(8,128)(2,1)S(1)}, u32[]{:S(2)}, u32[]{:S(2)}) %collective-permute-start.66) | collective-permute-done | bytes 131104 | tf_op jit(solution)/shard_map/ppermute | solution.py:262
  419.5 6.8 %collective-permute-done.79 = f32[2,256]{1,0:T(2,128)S(1)} collective-permute-done((f32[2,256]{1,0:T(2,128)S(1)}, f32[2,256]{1,0:T(2,128)S(1)}, u32[]{:S(2)}, u32[]{:S(2)}) %collective-permute-start.79) | collective-permute-done | bytes 2080 | tf_op jit(solution)/shard_map/ppermute | solution.py:262
  429.7 5.2 %collective-permute-start.81 = (bf16[4,128,256]{2,1,0:T(8,128)(2,1)}, bf16[4,128,256]{2,1,0:T(8,128)(2,1)}, u32[]{:S(2)}, u32[]{:S(2)}) collective-permute-start(bf16[4,128,256]{2,1,0:T(8,128)(2,1)} %fusion.90), channel_id=1, source_target_pairs={{0,1},{1,0},{2,3},{3,2},{4,5},{5,4},{6,7},{7,6},{8,9},{9,8},{10,11... | collective-permute-start | bytes 786440 | tf_op jit(solution)/shard_map/ppermute | solution.py:262
  (391 shorter events, 223.8 us)
Async XLA Ops:
  15.1 36.6 %collective-permute-start = (bf16[4,128,256]{2,1,0:T(8,128)(2,1)S(1)}, bf16[4,128,256]{2,1,0:T(8,128)(2,1)S(1)}, u32[]{:S(2)}, u32[]{:S(2)}) collective-permute-start(bf16[4,128,256]{2,1,0:T(8,128)(2,1)S(1)} %pad_maximum_fusion.16.refs_0_), channel_id=1, source_target_pairs={{0,4},{4,0},{8,12},{12,8},{1,5},{5,1},{9,13},{13,9},{2,6},{6,2},{1... | collective-permute-start | bytes 786440 | tf_op jit(solution)/shard_map/ppermute | solution.py:262
  17.3 32.4 %collective-permute-start.3 = (bf16[4,128,256]{2,1,0:T(8,128)(2,1)S(1)}, bf16[4,128,256]{2,1,0:T(8,128)(2,1)S(1)}, u32[]{:S(2)}, u32[]{:S(2)}) collective-permute-start(bf16[4,128,256]{2,1,0:T(8,128)(2,1)S(1)} %collective-permute-done.1.refs_1_), channel_id=1, source_target_pairs={{0,3},{1,2},{2,1},{3,0},{4,7},{5,6},{6,5},{7,4},{8,11},{9,10},{10,... | collective-permute-start | bytes 786440 | tf_op jit(solution)/shard_map/ppermute | solution.py:262
  64.4 28.0 %collective-permute-start.12 = (bf16[3,352,256]{2,1,0:T(8,128)(2,1)}, bf16[3,352,256]{2,1,0:T(8,128)(2,1)}, u32[]{:S(2)}, u32[]{:S(2)}) collective-permute-start(bf16[3,352,256]{2,1,0:T(8,128)(2,1)} %pad_maximum_fusion.7.refs_0_), channel_id=1, source_target_pairs={{0,1},{1,0},{2,3},{3,2},{4,5},{5,4},{6,7},{7,6},{8,9},{9,8},{10,11... | collective-permute-start | bytes 1622024 | tf_op jit(solution)/shard_map/ppermute | solution.py:262
  67.6 25.7 %collective-permute-start.35 = (bf16[256,1024]{1,0:T(8,128)(2,1)S(1)}, bf16[256,1024]{1,0:T(8,128)(2,1)S(1)}, u32[]{:S(2)}, u32[]{:S(2)}) collective-permute-start(bf16[256,1024]{1,0:T(8,128)(2,1)S(1)} %constant_dynamic-update-slice_fusion), channel_id=1, source_target_pairs={{0,16},{16,0},{1,17},{17,1},{2,18},{18,2},{3,19},{19,3},{4,20},{20... | collective-permute-start | bytes 1572872 | tf_op jit(solution)/shard_map/ppermute | solution.py:258
  83.7 41.0 %collective-permute-start.11 = (bf16[3,352,256]{2,1,0:T(8,128)(2,1)}, bf16[3,352,256]{2,1,0:T(8,128)(2,1)}, u32[]{:S(2)}, u32[]{:S(2)}) collective-permute-start(bf16[3,352,256]{2,1,0:T(8,128)(2,1)} %pad_maximum_fusion.7.refs_0_), channel_id=1, source_target_pairs={{0,4},{4,0},{8,12},{12,8},{1,5},{5,1},{9,13},{13,9},{2,6},{6,2},{1... | collective-permute-start | bytes 1622024 | tf_op jit(solution)/shard_map/ppermute | solution.py:262
  86.0 40.1 %collective-permute-start.18 = (bf16[3,352,256]{2,1,0:T(8,128)(2,1)}, bf16[3,352,256]{2,1,0:T(8,128)(2,1)}, u32[]{:S(2)}, u32[]{:S(2)}) collective-permute-start(bf16[3,352,256]{2,1,0:T(8,128)(2,1)} %pad_maximum_fusion.7.refs_0_), channel_id=1, source_target_pairs={{0,8},{4,12},{8,0},{12,4},{1,9},{5,13},{9,1},{13,5},{2,10},{6,14},... | collective-permute-start | bytes 1622024 | tf_op jit(solution)/shard_map/ppermute | solution.py:262
  93.7 33.1 %collective-permute-start.13 = (bf16[3,352,256]{2,1,0:T(8,128)(2,1)}, bf16[3,352,256]{2,1,0:T(8,128)(2,1)}, u32[]{:S(2)}, u32[]{:S(2)}) collective-permute-start(bf16[3,352,256]{2,1,0:T(8,128)(2,1)} %collective-permute-done.12.refs_1_), channel_id=1, source_target_pairs={{0,4},{4,0},{8,12},{12,8},{1,5},{5,1},{9,13},{13,9},{2,6},{6,2},{1... | collective-permute-start | bytes 1622024 | tf_op jit(solution)/shard_map/ppermute | solution.py:262
  97.4 30.9 %collective-permute-start.19 = (bf16[3,352,256]{2,1,0:T(8,128)(2,1)}, bf16[3,352,256]{2,1,0:T(8,128)(2,1)}, u32[]{:S(2)}, u32[]{:S(2)}) collective-permute-start(bf16[3,352,256]{2,1,0:T(8,128)(2,1)} %collective-permute-done.12.refs_1_), channel_id=1, source_target_pairs={{0,8},{4,12},{8,0},{12,4},{1,9},{5,13},{9,1},{13,5},{2,10},{6,14},... | collective-permute-start | bytes 1622024 | tf_op jit(solution)/shard_map/ppermute | solution.py:262
  128.3 92.7 %collective-permute-start.45 = (f32[512,1024]{1,0:T(8,128)S(1)}, f32[512,1024]{1,0:T(8,128)}, u32[]{:S(2)}, u32[]{:S(2)}) collective-permute-start(f32[512,1024]{1,0:T(8,128)S(1)} %fusion.99), channel_id=1, source_target_pairs={{0,16},{16,0},{1,17},{17,1},{2,18},{18,2},{3,19},{19,3},{4,20},{20... | collective-permute-start | bytes 6291464 | tf_op jit(solution)/shard_map/ppermute | solution.py:258
  149.1 39.9 %collective-permute-start.27 = (bf16[3,352,256]{2,1,0:T(8,128)(2,1)}, bf16[3,352,256]{2,1,0:T(8,128)(2,1)}, u32[]{:S(2)}, u32[]{:S(2)}) collective-permute-start(bf16[3,352,256]{2,1,0:T(8,128)(2,1)} %collective-permute-done.11.refs_4_), channel_id=1, source_target_pairs={{0,8},{4,12},{8,0},{12,4},{1,9},{5,13},{9,1},{13,5},{2,10},{6,14},... | collective-permute-start | bytes 1622024 | tf_op jit(solution)/shard_map/ppermute | solution.py:262
  151.0 25.9 %collective-permute-start.25 = (bf16[256,256]{1,0:T(8,128)(2,1)S(1)}, bf16[256,256]{1,0:T(8,128)(2,1)S(1)}, u32[]{:S(2)}, u32[]{:S(2)}) collective-permute-start(bf16[256,256]{1,0:T(8,128)(2,1)S(1)} %get-tuple-element.211), channel_id=1, source_target_pairs={{0,3},{1,2},{2,1},{3,0},{4,7},{5,6},{6,5},{7,4},{8,11},{9,10},{10,... | collective-permute-start | bytes 393224 | tf_op jit(solution)/shard_map/ppermute | solution.py:262
  153.8 32.3 %collective-permute-start.24 = (bf16[256,256]{1,0:T(8,128)(2,1)S(1)}, bf16[256,256]{1,0:T(8,128)(2,1)S(1)}, u32[]{:S(2)}, u32[]{:S(2)}) collective-permute-start(bf16[256,256]{1,0:T(8,128)(2,1)S(1)} %get-tuple-element.210), channel_id=1, source_target_pairs={{0,2},{1,3},{2,0},{3,1},{4,6},{5,7},{6,4},{7,5},{8,10},{9,11},{10,... | collective-permute-start | bytes 393224 | tf_op jit(solution)/shard_map/ppermute | solution.py:262
  189.0 30.5 %collective-permute-start.26 = (bf16[256,1024]{1,0:T(8,128)(2,1)}, bf16[256,1024]{1,0:T(8,128)(2,1)}, u32[]{:S(2)}, u32[]{:S(2)}) collective-permute-start(bf16[256,1024]{1,0:T(8,128)(2,1)} %pad_maximum_fusion.8), channel_id=1, source_target_pairs={{0,16},{16,0},{1,17},{17,1},{2,18},{18,2},{3,19},{19,3},{4,20},{20... | collective-permute-start | bytes 1572872 | tf_op jit(solution)/shard_map/ppermute | solution.py:258
  244.9 34.3 %collective-permute-start.46 = (bf16[2,2,352,512]{3,2,0,1:T(8,128)(2,1)}, bf16[2,2,352,512]{3,2,0,1:T(8,128)(2,1)}, u32[]{:S(2)}, u32[]{:S(2)}) collective-permute-start(bf16[2,2,352,512]{3,2,0,1:T(8,128)(2,1)} %copy_bitcast_fusion.1), channel_id=1, source_target_pairs={{0,8},{4,12},{8,0},{12,4},{1,9},{5,13},{9,1},{13,5},{2,10},{6,14},... | collective-permute-start | bytes 4325384 | tf_op jit(solution)/shard_map/ppermute | solution.py:262
  247.5 34.0 %collective-permute-start.47 = (bf16[2,2,352,512]{3,2,0,1:T(8,128)(2,1)}, bf16[2,2,352,512]{3,2,0,1:T(8,128)(2,1)}, u32[]{:S(2)}, u32[]{:S(2)}) collective-permute-start(bf16[2,2,352,512]{3,2,0,1:T(8,128)(2,1)} %copy_bitcast_fusion), channel_id=1, source_target_pairs={{0,4},{4,0},{8,12},{12,8},{1,5},{5,1},{9,13},{13,9},{2,6},{6,2},{1... | collective-permute-start | bytes 4325384 | tf_op jit(solution)/shard_map/ppermute | solution.py:262
  251.8 66.7 %collective-permute-start.56 = (bf16[1408,256]{1,0:T(8,128)(2,1)}, bf16[1408,256]{1,0:T(8,128)(2,1)}, u32[]{:S(2)}, u32[]{:S(2)}) collective-permute-start(bf16[1408,256]{1,0:T(8,128)(2,1)} %get-tuple-element.162), channel_id=1, source_target_pairs={{0,1},{1,0},{2,3},{3,2},{4,5},{5,4},{6,7},{7,6},{8,9},{9,8},{10,11... | collective-permute-start | bytes 2162696 | tf_op jit(solution)/shard_map/ppermute | solution.py:262
  251.8 66.8 %collective-permute-start.57 = (bf16[1408,256]{1,0:T(8,128)(2,1)}, bf16[1408,256]{1,0:T(8,128)(2,1)}, u32[]{:S(2)}, u32[]{:S(2)}) collective-permute-start(bf16[1408,256]{1,0:T(8,128)(2,1)} %get-tuple-element.161), channel_id=1, source_target_pairs={{0,2},{1,3},{2,0},{3,1},{4,6},{5,7},{6,4},{7,5},{8,10},{9,11},{10,... | collective-permute-start | bytes 2162696 | tf_op jit(solution)/shard_map/ppermute | solution.py:262
  301.2 35.4 %collective-permute-start.61 = (bf16[4,2,128,512]{3,2,0,1:T(8,128)(2,1)S(1)}, bf16[4,2,128,512]{3,2,0,1:T(8,128)(2,1)S(1)}, u32[]{:S(2)}, u32[]{:S(2)}) collective-permute-start(bf16[4,2,128,512]{3,2,0,1:T(8,128)(2,1)S(1)} %copy_bitcast_fusion.3), channel_id=1, source_target_pairs={{0,8},{4,12},{8,0},{12,4},{1,9},{5,13},{9,1},{13,5},{2,10},{6,14},... | collective-permute-start | bytes 3145736 | tf_op jit(solution)/shard_map/ppermute | solution.py:262
  318.6 85.0 %collective-permute-start.53 = (bf16[2,352,256]{2,1,0:T(8,128)(2,1)S(1)}, bf16[2,352,256]{2,1,0:T(8,128)(2,1)S(1)}, u32[]{:S(2)}, u32[]{:S(2)}) collective-permute-start(bf16[2,352,256]{2,1,0:T(8,128)(2,1)S(1)} %fusion.89), channel_id=1, source_target_pairs={{0,1},{1,0},{2,3},{3,2},{4,5},{5,4},{6,7},{7,6},{8,9},{9,8},{10,11... | collective-permute-start | bytes 1081352 | tf_op jit(solution)/shard_map/ppermute | solution.py:262
  355.9 47.6 %collective-permute-start.54 = (bf16[2,352,256]{2,1,0:T(8,128)(2,1)S(1)}, bf16[2,352,256]{2,1,0:T(8,128)(2,1)S(1)}, u32[]{:S(2)}, u32[]{:S(2)}) collective-permute-start(bf16[2,352,256]{2,1,0:T(8,128)(2,1)S(1)} %get-tuple-element.181), channel_id=1, source_target_pairs={{0,2},{1,3},{2,0},{3,1},{4,6},{5,7},{6,4},{7,5},{8,10},{9,11},{10,... | collective-permute-start | bytes 1081352 | tf_op jit(solution)/shard_map/ppermute | solution.py:262
  355.9 47.6 %collective-permute-start.55 = (bf16[2,352,256]{2,1,0:T(8,128)(2,1)S(1)}, bf16[2,352,256]{2,1,0:T(8,128)(2,1)S(1)}, u32[]{:S(2)}, u32[]{:S(2)}) collective-permute-start(bf16[2,352,256]{2,1,0:T(8,128)(2,1)S(1)} %get-tuple-element.180), channel_id=1, source_target_pairs={{0,3},{1,2},{2,1},{3,0},{4,7},{5,6},{6,5},{7,4},{8,11},{9,10},{10,... | collective-permute-start | bytes 1081352 | tf_op jit(solution)/shard_map/ppermute | solution.py:262
  359.6 35.4 %collective-permute-start.66 = (bf16[256,256]{1,0:T(8,128)(2,1)S(1)}, bf16[256,256]{1,0:T(8,128)(2,1)S(1)}, u32[]{:S(2)}, u32[]{:S(2)}) collective-permute-start(bf16[256,256]{1,0:T(8,128)(2,1)S(1)} %get-tuple-element.201), channel_id=1, source_target_pairs={{0,2},{1,3},{2,0},{3,1},{4,6},{5,7},{6,4},{7,5},{8,10},{9,11},{10,... | collective-permute-start | bytes 393224 | tf_op jit(solution)/shard_map/ppermute | solution.py:262
  399.5 40.5 %collective-permute-start.83 = (bf16[4,128,256]{2,1,0:T(8,128)(2,1)S(1)}, bf16[4,128,256]{2,1,0:T(8,128)(2,1)}, u32[]{:S(2)}, u32[]{:S(2)}) collective-permute-start(bf16[4,128,256]{2,1,0:T(8,128)(2,1)S(1)} %get-tuple-element.198), channel_id=1, source_target_pairs={{0,3},{1,2},{2,1},{3,0},{4,7},{5,6},{6,5},{7,4},{8,11},{9,10},{10,... | collective-permute-start | bytes 786440 | tf_op jit(solution)/shard_map/ppermute | solution.py:262
  401.7 38.7 %collective-permute-start.82 = (bf16[4,128,256]{2,1,0:T(8,128)(2,1)}, bf16[4,128,256]{2,1,0:T(8,128)(2,1)}, u32[]{:S(2)}, u32[]{:S(2)}) collective-permute-start(bf16[4,128,256]{2,1,0:T(8,128)(2,1)} %get-tuple-element.199), channel_id=1, source_target_pairs={{0,2},{1,3},{2,0},{3,1},{4,6},{5,7},{6,4},{7,5},{8,10},{9,11},{10,... | collective-permute-start | bytes 786440 | tf_op jit(solution)/shard_map/ppermute | solution.py:262
  (120 other events, 1415.3 us)

commit v2 on v1

--- a/solution.py
+++ b/solution.py
@@ -354,7 +354,8 @@
     block_rows = block if first_rows is None else after(block, first_rows)
     near = hop(block_cols, "col", 1)
     far = hop(block_cols, "col", 3)
-    grid[0] = [block_rows, near, hop(near, "col", 3), far]
+    relayed = hop(near, "col", 3)
+    grid[0] = [block_rows, near, relayed, far]
     for at in (0, 1, 3, 2):
         grid[1][at] = hop(grid[0][at], "row", 1)
         grid[2][at] = hop(grid[0][at], "row", 2)
@@ -477,7 +478,8 @@
         [pick(w_gate_up, core, 2).transpose(1, 2, 0), pick(w_down, core)[None]], axis=0
     )
     ffn_grid = spread_weights(ffn_block, attn_grid[0], attn_grid[1] + attn_grid[2])
-    big_qkv, big_out = after(join_weights(attn_grid, (3, 1)), ffn_grid[0])
+    attn_wholes = join_weights(attn_grid, (3, 1))
+    big_qkv, big_out = after(attn_wholes, ffn_grid[0])
     grad_late = after(grad_out, ffn_grid[1] + ffn_grid[2])
     grad_chunks = send_chunks(grad_late, core, col, length)
     big_gate_up, big_down = join_weights(ffn_grid, (2, 1))
@@ -576,6 +578,9 @@
     gain_sums = gain_sums + swap(gain_sums)
     gain_sums = gain_sums + hop(gain_sums, "row", 1)
     gain_sums = gain_sums + hop(gain_sums, "row", 2)
+    whole_gate_up = joined(mine_gate_up, core)
+    whole_down = joined(mine_down, core)
+    gain_sums = after(gain_sums, (whole_gate_up, whole_down))
     gain_mine = gain_sums[:, :features]
     for flip in range(1, 4):
         piece = gain_sums[:, flip * features : (flip + 1) * features]
@@ -589,8 +594,8 @@
         gain_mine[1],
         whole_attn[:3].transpose(2, 0, 1),
         whole_attn[3],
-        joined(mine_gate_up, core).transpose(2, 0, 1),
-        joined(mine_down, core)[0],
+        whole_gate_up.transpose(2, 0, 1),
+        whole_down[0],
     )
 
 

time: 461 us -> 456 us (0.989)
  starting transfers between devices: 138 us -> 133 us
    ppermute x71, starting transfers between devices: 136 us -> 131 us  [hop(): lax.ppermute(values, axis, [(at, at ^ flip) for at in range(lax.axis_size...]
  transfers between devices with their start and end apart: 87 -> 87, of which waited for: 32 -> 30; matrix products, arithmetic and copies ran while one was open for 18% -> 18% of each run, Pallas kernels for 4% -> 4%
where the time goes in v2:
time: 456 us; the launch traced here: 451 us
  waiting for transfers between devices  189 us (41%)
  starting transfers between devices  133 us (29%)
  matrix products  45.4 us (10%)
  other arithmetic  31.9 us (7%)
  local copies, waits for them, and re-layouts  29.4 us (6%)
  Pallas kernels  19.4 us (4%)
    ppermute x71, waiting for transfers between devices, hop(): lax.ppermute(values, axis, [(at, at ^ flip) for at in range(lax.axis_size...  188 us
    ppermute x71, starting transfers between devices, hop(): lax.ppermute(values, axis, [(at, at ^ flip) for at in range(lax.axis_size...  131 us
    pallas_call x2, Pallas kernels, join_weights(): pl.pallas_call(join_blocks, out_shape=shapes)  12.8 us
    dot_general x4, matrix products, times_t(): lax.dot_general(left, right, (((1,), (1,)), ((), ())), preferred_element_...  10.9 us
    unnamed x119, local copies, waits for them, and re-layouts  9.6 us
    convert_element_type x10, other arithmetic, low(): return values.astype(jnp.bfloat16)  9.44 us
  transfers between devices with their start and end apart: 87, of which 30 were waited for; matrix products, arithmetic and copies ran while one was open for 18% of the time, Pallas kernels for 4%

profile of v2, /device:TPU:0, one launch (start us, length us, event | category | flops | bytes accessed | tf_op | source)
XLA Modules:
  0.0 450.7 jit_solution(11250853484455924236)
XLA Ops:
  1.5 5.1 %collective-permute-start.38 = (f32[2,256]{1,0:T(2,128)S(1)}, f32[2,256]{1,0:T(2,128)S(1)}, u32[]{:S(2)}, u32[]{:S(2)}) collective-permute-start(f32[2,256]{1,0:T(2,128)S(1)} %pad_maximum_fusion.23), channel_id=1, source_target_pairs={{0,3},{1,2},{2,1},{3,0},{4,7},{5,6},{6,5},{7,4},{8,11},{9,10},{10,... | collective-permute-start | bytes 6152 | tf_op jit(solution)/shard_map/ppermute | solution.py:262
  17.3 8.6 %collective-permute-start.3 = (bf16[4,128,256]{2,1,0:T(8,128)(2,1)S(1)}, bf16[4,128,256]{2,1,0:T(8,128)(2,1)S(1)}, u32[]{:S(2)}, u32[]{:S(2)}) collective-permute-start(bf16[4,128,256]{2,1,0:T(8,128)(2,1)S(1)} %collective-permute-done.1.refs_1_), channel_id=1, source_target_pairs={{0,3},{1,2},{2,1},{3,0},{4,7},{5,6},{6,5},{7,4},{8,11},{9,10},{10,... | collective-permute-start | bytes 786440 | tf_op jit(solution)/shard_map/ppermute | solution.py:262
  26.3 10.2 %collective-permute-start.33 = (bf16[256,256]{1,0:T(8,128)(2,1)S(1)}, bf16[256,256]{1,0:T(8,128)(2,1)S(1)}, u32[]{:S(2)}, u32[]{:S(2)}) collective-permute-start(bf16[256,256]{1,0:T(8,128)(2,1)S(1)} %get-tuple-element.209), channel_id=1, source_target_pairs={{0,2},{1,3},{2,0},{3,1},{4,6},{5,7},{6,4},{7,5},{8,10},{9,11},{10,... | collective-permute-start | bytes 393224 | tf_op jit(solution)/shard_map/ppermute | solution.py:262
  39.6 8.6 %collective-permute-done.33 = bf16[256,256]{1,0:T(8,128)(2,1)S(1)} collective-permute-done((bf16[256,256]{1,0:T(8,128)(2,1)S(1)}, bf16[256,256]{1,0:T(8,128)(2,1)S(1)}, u32[]{:S(2)}, u32[]{:S(2)}) %collective-permute-start.33) | collective-permute-done | bytes 131104 | tf_op jit(solution)/shard_map/ppermute | solution.py:262
  58.9 4.1 collective-permute-done.6.refs_7_
  87.7 4.7 %shard_map.153 = (bf16[3,512,1024]{2,1,0:T(8,128)(2,1)}, bf16[1,512,1024]{2,1,0:T(8,128)(2,1)}) custom-call(bf16[4,128,256]{2,1,0:T(8,128)(2,1)} %copy-done.12, bf16[4,128,256]{2,1,0:T(8,128)(2,1)} %copy-done.26, bf16[4,128,256]{2,1,0:T(8,128)(2,1)} %copy-done.29, bf16[4,128,256]{2,1,0:T(8,128)(2,1)} %copy-done.27, bf16[4,128,256]{2,1,0:T(8,128)(2,1)} %copy-done.28, ...), custom_call_target="tpu_custom_call" | custom-call | tf_op jit(solution)/shard_map/pallas_call | solution.py:373
  99.6 8.3 %collective-permute-done.14.refs_2_ = bf16[3,352,256]{2,1,0:T(8,128)(2,1)S(1)} collective-permute-done((bf16[3,352,256]{2,1,0:T(8,128)(2,1)}, bf16[3,352,256]{2,1,0:T(8,128)(2,1)S(1)}, u32[]{:S(2)}, u32[]{:S(2)}) %collective-permute-start.14) | collective-permute-done | bytes 540704 | tf_op jit(solution)/shard_map/ppermute | solution.py:262
  114.7 5.5 %fusion.96 = (f32[8,512]{1,0:T(8,128)S(1)}, f32[8,512,512]{1,2,0:T(8,128)}) fusion(pred[512,512]{0,1:T(8,128)(4,1)S(1)} %copy-done.41, bf16[512,3,8,64]{0,3,2,1:T(8,128)(2,1)S(1)} %bitcast.226), kind=kOutput, calls=%fused_computation.233 | convolution fusion | flops 276824576 | bytes 9715712 | tf_op jit(solution)/shard_map/sub | solution.py:497
  120.3 4.4 fusion.28
  128.4 11.8 %collective-permute-done.21.refs_11_ = bf16[3,352,256]{2,1,0:T(8,128)(2,1)} collective-permute-done((bf16[3,352,256]{2,1,0:T(8,128)(2,1)}, bf16[3,352,256]{2,1,0:T(8,128)(2,1)}, u32[]{:S(2)}, u32[]{:S(2)}) %collective-permute-start.21) | collective-permute-done | bytes 540704 | tf_op jit(solution)/shard_map/ppermute | solution.py:262
  140.2 8.8 %collective-permute-done.20.refs_10_ = bf16[3,352,256]{2,1,0:T(8,128)(2,1)} collective-permute-done((bf16[3,352,256]{2,1,0:T(8,128)(2,1)S(1)}, bf16[3,352,256]{2,1,0:T(8,128)(2,1)}, u32[]{:S(2)}, u32[]{:S(2)}) %collective-permute-start.20) | collective-permute-done | bytes 540704 | tf_op jit(solution)/shard_map/ppermute | solution.py:262
  153.8 23.2 %collective-permute-start.24 = (bf16[256,256]{1,0:T(8,128)(2,1)S(1)}, bf16[256,256]{1,0:T(8,128)(2,1)S(1)}, u32[]{:S(2)}, u32[]{:S(2)}) collective-permute-start(bf16[256,256]{1,0:T(8,128)(2,1)S(1)} %get-tuple-element.212), channel_id=1, source_target_pairs={{0,2},{1,3},{2,0},{3,1},{4,6},{5,7},{6,4},{7,5},{8,10},{9,11},{10,... | collective-permute-start | bytes 393224 | tf_op jit(solution)/shard_map/ppermute | solution.py:262
  178.3 7.8 %collective-permute-done.24 = bf16[256,256]{1,0:T(8,128)(2,1)S(1)} collective-permute-done((bf16[256,256]{1,0:T(8,128)(2,1)S(1)}, bf16[256,256]{1,0:T(8,128)(2,1)S(1)}, u32[]{:S(2)}, u32[]{:S(2)}) %collective-permute-start.24) | collective-permute-done | bytes 131104 | tf_op jit(solution)/shard_map/ppermute | solution.py:262
  191.0 10.5 %collective-permute-done.30.refs_15_ = bf16[3,352,256]{2,1,0:T(8,128)(2,1)} collective-permute-done((bf16[3,352,256]{2,1,0:T(8,128)(2,1)}, bf16[3,352,256]{2,1,0:T(8,128)(2,1)}, u32[]{:S(2)}, u32[]{:S(2)}) %collective-permute-start.30) | collective-permute-done | bytes 540704 | tf_op jit(solution)/shard_map/ppermute | solution.py:262
  201.5 9.9 %collective-permute-done.29.refs_14_ = bf16[3,352,256]{2,1,0:T(8,128)(2,1)} collective-permute-done((bf16[3,352,256]{2,1,0:T(8,128)(2,1)}, bf16[3,352,256]{2,1,0:T(8,128)(2,1)}, u32[]{:S(2)}, u32[]{:S(2)}) %collective-permute-start.29) | collective-permute-done | bytes 540704 | tf_op jit(solution)/shard_map/ppermute | solution.py:262
  211.4 8.1 %shard_map.152 = (bf16[2,1408,1024]{2,1,0:T(8,128)(2,1)}, bf16[1,1408,1024]{2,1,0:T(8,128)(2,1)}) custom-call(bf16[3,352,256]{2,1,0:T(8,128)(2,1)} %pad_maximum_fusion.7.refs_0_, bf16[3,352,256]{2,1,0:T(8,128)(2,1)} %collective-permute-done.12.refs_1_, bf16[3,352,256]{2,1,0:T(8,128)(2,1)} %copy-done.17, ...), custom_call_target="tpu_custom_call" | custom-call | tf_op jit(solution)/shard_map/pallas_call | solution.py:373
  235.3 3.7 convolution_convert_fusion
  273.7 5.4 %collective-permute-done.46 = bf16[2,2,352,512]{3,2,0,1:T(8,128)(2,1)} collective-permute-done((bf16[2,2,352,512]{3,2,0,1:T(8,128)(2,1)}, bf16[2,2,352,512]{3,2,0,1:T(8,128)(2,1)}, u32[]{:S(2)}, u32[]{:S(2)}) %collective-permute-start.46) | collective-permute-done | bytes 1441824 | tf_op jit(solution)/shard_map/ppermute | solution.py:262
  301.9 12.7 %collective-permute-done.50 = bf16[2,352,512]{2,1,0:T(8,128)(2,1)S(1)} collective-permute-done((bf16[2,352,512]{2,1,0:T(8,128)(2,1)S(1)}, bf16[2,352,512]{2,1,0:T(8,128)(2,1)S(1)}, u32[]{:S(2)}, u32[]{:S(2)}) %collective-permute-start.50) | collective-permute-done | bytes 720928 | tf_op jit(solution)/shard_map/ppermute | solution.py:262
  320.5 16.1 %collective-permute-done.61 = bf16[4,2,128,512]{3,2,0,1:T(8,128)(2,1)S(1)} collective-permute-done((bf16[4,2,128,512]{3,2,0,1:T(8,128)(2,1)S(1)}, bf16[4,2,128,512]{3,2,0,1:T(8,128)(2,1)S(1)}, u32[]{:S(2)}, u32[]{:S(2)}) %collective-permute-start.61) | collective-permute-done | bytes 1048608 | tf_op jit(solution)/shard_map/ppermute | solution.py:262
  343.4 12.6 %collective-permute-done.59 = bf16[1,2,352,128]{3,2,1,0:T(8,128)(2,1)S(1)} collective-permute-done((bf16[1,2,352,128]{3,2,1,0:T(8,128)(2,1)S(1)}, bf16[1,2,352,128]{3,2,1,0:T(8,128)(2,1)S(1)}, u32[]{:S(2)}, u32[]{:S(2)}) %collective-permute-start.59) | collective-permute-done | bytes 180256 | tf_op jit(solution)/shard_map/ppermute | solution.py:262
  361.2 13.4 %collective-permute-done.65 = bf16[256,256]{1,0:T(8,128)(2,1)S(1)} collective-permute-done((bf16[256,256]{1,0:T(8,128)(2,1)S(1)}, bf16[256,256]{1,0:T(8,128)(2,1)S(1)}, u32[]{:S(2)}, u32[]{:S(2)}) %collective-permute-start.65) | collective-permute-done | bytes 131104 | tf_op jit(solution)/shard_map/ppermute | solution.py:262
  377.1 17.9 %collective-permute-done.66 = bf16[256,256]{1,0:T(8,128)(2,1)S(1)} collective-permute-done((bf16[256,256]{1,0:T(8,128)(2,1)S(1)}, bf16[256,256]{1,0:T(8,128)(2,1)S(1)}, u32[]{:S(2)}, u32[]{:S(2)}) %collective-permute-start.66) | collective-permute-done | bytes 131104 | tf_op jit(solution)/shard_map/ppermute | solution.py:262
  425.1 11.3 %collective-permute-done.84 = bf16[4,128,256]{2,1,0:T(8,128)(2,1)} collective-permute-done((bf16[4,128,256]{2,1,0:T(8,128)(2,1)}, bf16[4,128,256]{2,1,0:T(8,128)(2,1)}, u32[]{:S(2)}, u32[]{:S(2)}) %collective-permute-start.84) | collective-permute-done | bytes 262176 | tf_op jit(solution)/shard_map/ppermute | solution.py:262
  (391 shorter events, 215.9 us)
Async XLA Ops:
  15.1 36.6 %collective-permute-start = (bf16[4,128,256]{2,1,0:T(8,128)(2,1)S(1)}, bf16[4,128,256]{2,1,0:T(8,128)(2,1)S(1)}, u32[]{:S(2)}, u32[]{:S(2)}) collective-permute-start(bf16[4,128,256]{2,1,0:T(8,128)(2,1)S(1)} %pad_maximum_fusion.16.refs_0_), channel_id=1, source_target_pairs={{0,4},{4,0},{8,12},{12,8},{1,5},{5,1},{9,13},{13,9},{2,6},{6,2},{1... | collective-permute-start | bytes 786440 | tf_op jit(solution)/shard_map/ppermute | solution.py:262
  17.3 32.4 %collective-permute-start.3 = (bf16[4,128,256]{2,1,0:T(8,128)(2,1)S(1)}, bf16[4,128,256]{2,1,0:T(8,128)(2,1)S(1)}, u32[]{:S(2)}, u32[]{:S(2)}) collective-permute-start(bf16[4,128,256]{2,1,0:T(8,128)(2,1)S(1)} %collective-permute-done.1.refs_1_), channel_id=1, source_target_pairs={{0,3},{1,2},{2,1},{3,0},{4,7},{5,6},{6,5},{7,4},{8,11},{9,10},{10,... | collective-permute-start | bytes 786440 | tf_op jit(solution)/shard_map/ppermute | solution.py:262
  64.4 28.0 %collective-permute-start.12 = (bf16[3,352,256]{2,1,0:T(8,128)(2,1)}, bf16[3,352,256]{2,1,0:T(8,128)(2,1)}, u32[]{:S(2)}, u32[]{:S(2)}) collective-permute-start(bf16[3,352,256]{2,1,0:T(8,128)(2,1)} %pad_maximum_fusion.7.refs_0_), channel_id=1, source_target_pairs={{0,1},{1,0},{2,3},{3,2},{4,5},{5,4},{6,7},{7,6},{8,9},{9,8},{10,11... | collective-permute-start | bytes 1622024 | tf_op jit(solution)/shard_map/ppermute | solution.py:262
  67.6 25.7 %collective-permute-start.35 = (bf16[256,1024]{1,0:T(8,128)(2,1)S(1)}, bf16[256,1024]{1,0:T(8,128)(2,1)S(1)}, u32[]{:S(2)}, u32[]{:S(2)}) collective-permute-start(bf16[256,1024]{1,0:T(8,128)(2,1)S(1)} %constant_dynamic-update-slice_fusion), channel_id=1, source_target_pairs={{0,16},{16,0},{1,17},{17,1},{2,18},{18,2},{3,19},{19,3},{4,20},{20... | collective-permute-start | bytes 1572872 | tf_op jit(solution)/shard_map/ppermute | solution.py:258
  83.7 41.0 %collective-permute-start.11 = (bf16[3,352,256]{2,1,0:T(8,128)(2,1)}, bf16[3,352,256]{2,1,0:T(8,128)(2,1)}, u32[]{:S(2)}, u32[]{:S(2)}) collective-permute-start(bf16[3,352,256]{2,1,0:T(8,128)(2,1)} %pad_maximum_fusion.7.refs_0_), channel_id=1, source_target_pairs={{0,4},{4,0},{8,12},{12,8},{1,5},{5,1},{9,13},{13,9},{2,6},{6,2},{1... | collective-permute-start | bytes 1622024 | tf_op jit(solution)/shard_map/ppermute | solution.py:262
  86.0 40.1 %collective-permute-start.18 = (bf16[3,352,256]{2,1,0:T(8,128)(2,1)}, bf16[3,352,256]{2,1,0:T(8,128)(2,1)}, u32[]{:S(2)}, u32[]{:S(2)}) collective-permute-start(bf16[3,352,256]{2,1,0:T(8,128)(2,1)} %pad_maximum_fusion.7.refs_0_), channel_id=1, source_target_pairs={{0,8},{4,12},{8,0},{12,4},{1,9},{5,13},{9,1},{13,5},{2,10},{6,14},... | collective-permute-start | bytes 1622024 | tf_op jit(solution)/shard_map/ppermute | solution.py:262
  93.7 33.1 %collective-permute-start.13 = (bf16[3,352,256]{2,1,0:T(8,128)(2,1)}, bf16[3,352,256]{2,1,0:T(8,128)(2,1)}, u32[]{:S(2)}, u32[]{:S(2)}) collective-permute-start(bf16[3,352,256]{2,1,0:T(8,128)(2,1)} %collective-permute-done.12.refs_1_), channel_id=1, source_target_pairs={{0,4},{4,0},{8,12},{12,8},{1,5},{5,1},{9,13},{13,9},{2,6},{6,2},{1... | collective-permute-start | bytes 1622024 | tf_op jit(solution)/shard_map/ppermute | solution.py:262
  97.4 30.9 %collective-permute-start.19 = (bf16[3,352,256]{2,1,0:T(8,128)(2,1)}, bf16[3,352,256]{2,1,0:T(8,128)(2,1)}, u32[]{:S(2)}, u32[]{:S(2)}) collective-permute-start(bf16[3,352,256]{2,1,0:T(8,128)(2,1)} %collective-permute-done.12.refs_1_), channel_id=1, source_target_pairs={{0,8},{4,12},{8,0},{12,4},{1,9},{5,13},{9,1},{13,5},{2,10},{6,14},... | collective-permute-start | bytes 1622024 | tf_op jit(solution)/shard_map/ppermute | solution.py:262
  128.3 92.7 %collective-permute-start.45 = (f32[512,1024]{1,0:T(8,128)S(1)}, f32[512,1024]{1,0:T(8,128)}, u32[]{:S(2)}, u32[]{:S(2)}) collective-permute-start(f32[512,1024]{1,0:T(8,128)S(1)} %fusion.97), channel_id=1, source_target_pairs={{0,16},{16,0},{1,17},{17,1},{2,18},{18,2},{3,19},{19,3},{4,20},{20... | collective-permute-start | bytes 6291464 | tf_op jit(solution)/shard_map/ppermute | solution.py:258
  149.1 39.9 %collective-permute-start.27 = (bf16[3,352,256]{2,1,0:T(8,128)(2,1)}, bf16[3,352,256]{2,1,0:T(8,128)(2,1)}, u32[]{:S(2)}, u32[]{:S(2)}) collective-permute-start(bf16[3,352,256]{2,1,0:T(8,128)(2,1)} %collective-permute-done.11.refs_4_), channel_id=1, source_target_pairs={{0,8},{4,12},{8,0},{12,4},{1,9},{5,13},{9,1},{13,5},{2,10},{6,14},... | collective-permute-start | bytes 1622024 | tf_op jit(solution)/shard_map/ppermute | solution.py:262
  151.0 25.9 %collective-permute-start.25 = (bf16[256,256]{1,0:T(8,128)(2,1)S(1)}, bf16[256,256]{1,0:T(8,128)(2,1)S(1)}, u32[]{:S(2)}, u32[]{:S(2)}) collective-permute-start(bf16[256,256]{1,0:T(8,128)(2,1)S(1)} %get-tuple-element.213), channel_id=1, source_target_pairs={{0,3},{1,2},{2,1},{3,0},{4,7},{5,6},{6,5},{7,4},{8,11},{9,10},{10,... | collective-permute-start | bytes 393224 | tf_op jit(solution)/shard_map/ppermute | solution.py:262
  153.8 32.3 %collective-permute-start.24 = (bf16[256,256]{1,0:T(8,128)(2,1)S(1)}, bf16[256,256]{1,0:T(8,128)(2,1)S(1)}, u32[]{:S(2)}, u32[]{:S(2)}) collective-permute-start(bf16[256,256]{1,0:T(8,128)(2,1)S(1)} %get-tuple-element.212), channel_id=1, source_target_pairs={{0,2},{1,3},{2,0},{3,1},{4,6},{5,7},{6,4},{7,5},{8,10},{9,11},{10,... | collective-permute-start | bytes 393224 | tf_op jit(solution)/shard_map/ppermute | solution.py:262
  187.2 24.3 %collective-permute-start.29 = (bf16[3,352,256]{2,1,0:T(8,128)(2,1)}, bf16[3,352,256]{2,1,0:T(8,128)(2,1)}, u32[]{:S(2)}, u32[]{:S(2)}) collective-permute-start(bf16[3,352,256]{2,1,0:T(8,128)(2,1)} %collective-permute-done.20.refs_10_), channel_id=1, source_target_pairs={{0,4},{4,0},{8,12},{12,8},{1,5},{5,1},{9,13},{13,9},{2,6},{6,2},{1... | collective-permute-start | bytes 1622024 | tf_op jit(solution)/shard_map/ppermute | solution.py:262
  189.0 30.5 %collective-permute-start.26 = (bf16[256,1024]{1,0:T(8,128)(2,1)}, bf16[256,1024]{1,0:T(8,128)(2,1)}, u32[]{:S(2)}, u32[]{:S(2)}) collective-permute-start(bf16[256,1024]{1,0:T(8,128)(2,1)} %pad_maximum_fusion.8), channel_id=1, source_target_pairs={{0,16},{16,0},{1,17},{17,1},{2,18},{18,2},{3,19},{19,3},{4,20},{20... | collective-permute-start | bytes 1572872 | tf_op jit(solution)/shard_map/ppermute | solution.py:258
  244.9 34.3 %collective-permute-start.46 = (bf16[2,2,352,512]{3,2,0,1:T(8,128)(2,1)}, bf16[2,2,352,512]{3,2,0,1:T(8,128)(2,1)}, u32[]{:S(2)}, u32[]{:S(2)}) collective-permute-start(bf16[2,2,352,512]{3,2,0,1:T(8,128)(2,1)} %copy_bitcast_fusion.1), channel_id=1, source_target_pairs={{0,8},{4,12},{8,0},{12,4},{1,9},{5,13},{9,1},{13,5},{2,10},{6,14},... | collective-permute-start | bytes 4325384 | tf_op jit(solution)/shard_map/ppermute | solution.py:262
  247.5 34.0 %collective-permute-start.47 = (bf16[2,2,352,512]{3,2,0,1:T(8,128)(2,1)}, bf16[2,2,352,512]{3,2,0,1:T(8,128)(2,1)}, u32[]{:S(2)}, u32[]{:S(2)}) collective-permute-start(bf16[2,2,352,512]{3,2,0,1:T(8,128)(2,1)} %copy_bitcast_fusion), channel_id=1, source_target_pairs={{0,4},{4,0},{8,12},{12,8},{1,5},{5,1},{9,13},{13,9},{2,6},{6,2},{1... | collective-permute-start | bytes 4325384 | tf_op jit(solution)/shard_map/ppermute | solution.py:262
  251.8 66.7 %collective-permute-start.56 = (bf16[1408,256]{1,0:T(8,128)(2,1)}, bf16[1408,256]{1,0:T(8,128)(2,1)}, u32[]{:S(2)}, u32[]{:S(2)}) collective-permute-start(bf16[1408,256]{1,0:T(8,128)(2,1)} %get-tuple-element.164), channel_id=1, source_target_pairs={{0,1},{1,0},{2,3},{3,2},{4,5},{5,4},{6,7},{7,6},{8,9},{9,8},{10,11... | collective-permute-start | bytes 2162696 | tf_op jit(solution)/shard_map/ppermute | solution.py:262
  251.8 66.8 %collective-permute-start.57 = (bf16[1408,256]{1,0:T(8,128)(2,1)}, bf16[1408,256]{1,0:T(8,128)(2,1)}, u32[]{:S(2)}, u32[]{:S(2)}) collective-permute-start(bf16[1408,256]{1,0:T(8,128)(2,1)} %get-tuple-element.163), channel_id=1, source_target_pairs={{0,2},{1,3},{2,0},{3,1},{4,6},{5,7},{6,4},{7,5},{8,10},{9,11},{10,... | collective-permute-start | bytes 2162696 | tf_op jit(solution)/shard_map/ppermute | solution.py:262
  301.2 35.4 %collective-permute-start.61 = (bf16[4,2,128,512]{3,2,0,1:T(8,128)(2,1)S(1)}, bf16[4,2,128,512]{3,2,0,1:T(8,128)(2,1)S(1)}, u32[]{:S(2)}, u32[]{:S(2)}) collective-permute-start(bf16[4,2,128,512]{3,2,0,1:T(8,128)(2,1)S(1)} %copy_bitcast_fusion.3), channel_id=1, source_target_pairs={{0,8},{4,12},{8,0},{12,4},{1,9},{5,13},{9,1},{13,5},{2,10},{6,14},... | collective-permute-start | bytes 3145736 | tf_op jit(solution)/shard_map/ppermute | solution.py:262
  314.6 24.2 %collective-permute-start.62 = (bf16[4,2,128,512]{3,2,0,1:T(8,128)(2,1)S(1)}, bf16[4,2,128,512]{3,2,0,1:T(8,128)(2,1)S(1)}, u32[]{:S(2)}, u32[]{:S(2)}) collective-permute-start(bf16[4,2,128,512]{3,2,0,1:T(8,128)(2,1)S(1)} %copy_bitcast_fusion.2), channel_id=1, source_target_pairs={{0,4},{4,0},{8,12},{12,8},{1,5},{5,1},{9,13},{13,9},{2,6},{6,2},{1... | collective-permute-start | bytes 3145736 | tf_op jit(solution)/shard_map/ppermute | solution.py:262
  318.6 85.0 %collective-permute-start.53 = (bf16[2,352,256]{2,1,0:T(8,128)(2,1)S(1)}, bf16[2,352,256]{2,1,0:T(8,128)(2,1)S(1)}, u32[]{:S(2)}, u32[]{:S(2)}) collective-permute-start(bf16[2,352,256]{2,1,0:T(8,128)(2,1)S(1)} %fusion.87), channel_id=1, source_target_pairs={{0,1},{1,0},{2,3},{3,2},{4,5},{5,4},{6,7},{7,6},{8,9},{9,8},{10,11... | collective-permute-start | bytes 1081352 | tf_op jit(solution)/shard_map/ppermute | solution.py:262
  355.9 48.0 %collective-permute-start.54 = (bf16[2,352,256]{2,1,0:T(8,128)(2,1)S(1)}, bf16[2,352,256]{2,1,0:T(8,128)(2,1)S(1)}, u32[]{:S(2)}, u32[]{:S(2)}) collective-permute-start(bf16[2,352,256]{2,1,0:T(8,128)(2,1)S(1)} %get-tuple-element.183), channel_id=1, source_target_pairs={{0,2},{1,3},{2,0},{3,1},{4,6},{5,7},{6,4},{7,5},{8,10},{9,11},{10,... | collective-permute-start | bytes 1081352 | tf_op jit(solution)/shard_map/ppermute | solution.py:262
  355.9 48.0 %collective-permute-start.55 = (bf16[2,352,256]{2,1,0:T(8,128)(2,1)S(1)}, bf16[2,352,256]{2,1,0:T(8,128)(2,1)S(1)}, u32[]{:S(2)}, u32[]{:S(2)}) collective-permute-start(bf16[2,352,256]{2,1,0:T(8,128)(2,1)S(1)} %get-tuple-element.182), channel_id=1, source_target_pairs={{0,3},{1,2},{2,1},{3,0},{4,7},{5,6},{6,5},{7,4},{8,11},{9,10},{10,... | collective-permute-start | bytes 1081352 | tf_op jit(solution)/shard_map/ppermute | solution.py:262
  359.6 35.4 %collective-permute-start.66 = (bf16[256,256]{1,0:T(8,128)(2,1)S(1)}, bf16[256,256]{1,0:T(8,128)(2,1)S(1)}, u32[]{:S(2)}, u32[]{:S(2)}) collective-permute-start(bf16[256,256]{1,0:T(8,128)(2,1)S(1)} %get-tuple-element.203), channel_id=1, source_target_pairs={{0,2},{1,3},{2,0},{3,1},{4,6},{5,7},{6,4},{7,5},{8,10},{9,11},{10,... | collective-permute-start | bytes 393224 | tf_op jit(solution)/shard_map/ppermute | solution.py:262
  (120 other events, 1447.7 us)
